TPU v7x, 128 devices: a whole 4x4x4 slice. The times are simulated.
128 devices in a mesh: shot: 16 (over z, x_hi, core), tile: 8 (over x_lo, y).
Axes of the slice: x: 4 (x_hi: 2, x_lo: 2; x = x_hi * 2 + x_lo), y: 4, z: 4, core: 2. Of those that a mesh axis runs over, the one named last changes fastest.
Arguments:
- lame_lambda: float32 [512, 32, 256], P(('shot', 'tile')), may hold values from 1 to 2
- lame_mu: float32 [512, 32, 256], P(('shot', 'tile')), may hold values from 0.5 to 1
- buoyancy: float32 [512, 32, 256], P(('shot', 'tile')), may hold values from 0.5 to 1
- aperture_row: int32 [16], replicated, may hold values from 0 to 15
- wave_state: float32 [16, 9, 32, 32, 256], P('shot', None, 'tile'), may hold values from -6 to 6
- source_cell: int32 [16], P('shot'), may hold values from 0 to 262143
- wavelet: float32 [16, 12], P('shot'), may hold values from -12 to 12
- receiver_cell: int32 [16, 256], P('shot'), may hold values from 0 to 262143
- prev_row: int32 [16], replicated, may hold values from 0 to 15
- prev_grad: float32 [16, 32, 32, 256], P('shot', 'tile'), may hold values from -6 to 6
Outputs:
- final_state: float32 [16, 9, 32, 32, 256], P('shot', None, 'tile')
- image_sum: float32 [16, 32, 32, 256], P('shot', 'tile')
- owner_grad: float32 [512, 32, 256], P(('shot', 'tile'))
- traces: float32 [16, 12, 256], P('shot')
Inputs may be any that keep to these rules, and one draw needn't show every extreme that they name: `aperture_row`: row q of model tiles holds the cells with x from q * 32 to q * 32 + 31; several shots may share a row and some rows have none. `prev_row`: rows of the previous batch, in the same sense. `source_cell`: flat index x * 32 * 256 + y * 256 + z within the shot's aperture. `receiver_cell`: flat indices as for source_cell; two receivers may share a cell.
All inputs are finite; a program needn't handle non-finite values.
Results may differ from a plain program's by a relative error of at most 0.0003.
Values sent between devices are 32-bit elements; how exact they have to be, the bound alone decides.
A program may use at most 64 MiB of HBM per device.

v0:
```python
import jax
import jax.numpy as jnp
from jax import lax
from jax.sharding import PartitionSpec as P

coefficients = (0.8, -0.2, 4.0 / 105.0, -1.0 / 280.0)
time_step = 0.2


def extended(cells, sides, width):
    for axis, dim in sides:
        count = lax.axis_size(axis)
        ends = count - 1
        head = lax.slice_in_dim(cells, 0, width, axis=dim)
        tail = lax.slice_in_dim(cells, cells.shape[dim] - width, cells.shape[dim], axis=dim)
        cells = jnp.concatenate(
            [
                lax.ppermute(tail, axis, [(i, (i + 1) % count) for i in range(ends)]),
                cells,
                lax.ppermute(head, axis, [((i + 1) % count, i) for i in range(ends)]),
            ],
            axis=dim,
        )
    return cells


def central(padded, axis, length):
    result = None
    for neighbor in range(1, 5):
        forward = lax.slice_in_dim(padded, 4 + neighbor, 4 + neighbor + length, axis=axis)
        backward = lax.slice_in_dim(padded, 4 - neighbor, 4 - neighbor + length, axis=axis)
        term = coefficients[neighbor - 1] * (forward - backward)
        result = term if result is None else result + term
    return result


def derive(field, axis):
    widths = [(0, 0)] * field.ndim
    widths[axis] = (4, 4)
    return central(jnp.pad(field, widths), axis, field.shape[axis])


def inject(velocity_z, buoy_cells, where_local, amplitude):
    flat = velocity_z.reshape(-1)
    count = flat.shape[0]
    inside = (where_local >= 0) & (where_local < count)
    index_at = jnp.clip(where_local, 0, count - 1)
    added = jnp.where(inside, time_step * buoy_cells.reshape(-1)[index_at] * amplitude, 0.0)
    return flat.at[index_at].add(added).reshape(velocity_z.shape)


def sample_at(velocity_z, where_local):
    flat = velocity_z.reshape(-1)
    count = flat.shape[0]
    inside = (where_local >= 0) & (where_local < count)
    index_at = jnp.clip(where_local, 0, count - 1)
    return jnp.where(inside, flat[index_at], 0.0)


def pad_stress(stacked):
    return extended(stacked, (("tile", 1),), 4)


def pad_velocity(stacked):
    return extended(stacked, (("tile", 1),), 4)


def advance_fields(fields, buoy_cells, lambda_cells, shear_cells, source_local, amplitude):
    (
        velocity_x,
        velocity_y,
        velocity_z,
        stress_xx,
        stress_yy,
        stress_zz,
        stress_xy,
        stress_xz,
        stress_yz,
    ) = fields
    length = velocity_x.shape[0]
    stress_dx = central(pad_stress(jnp.stack([stress_xx, stress_xy, stress_xz])), 1, length)
    velocity_x = velocity_x + time_step * buoy_cells * (
        stress_dx[0] + derive(stress_xy, 1) + derive(stress_xz, 2)
    )
    velocity_y = velocity_y + time_step * buoy_cells * (
        stress_dx[1] + derive(stress_yy, 1) + derive(stress_yz, 2)
    )
    velocity_z = velocity_z + time_step * buoy_cells * (
        stress_dx[2] + derive(stress_yz, 1) + derive(stress_zz, 2)
    )
    velocity_z = inject(velocity_z, buoy_cells, source_local, amplitude)
    velocity_dx = central(pad_velocity(jnp.stack([velocity_x, velocity_y, velocity_z])), 1, length)
    strain_xx = velocity_dx[0]
    strain_yy = derive(velocity_y, 1)
    strain_zz = derive(velocity_z, 2)
    dilation = strain_xx + strain_yy + strain_zz
    stress_xx = stress_xx + time_step * (lambda_cells * dilation + 2.0 * shear_cells * strain_xx)
    stress_yy = stress_yy + time_step * (lambda_cells * dilation + 2.0 * shear_cells * strain_yy)
    stress_zz = stress_zz + time_step * (lambda_cells * dilation + 2.0 * shear_cells * strain_zz)
    stress_xy = stress_xy + time_step * shear_cells * (derive(velocity_x, 1) + velocity_dx[1])
    stress_xz = stress_xz + time_step * shear_cells * (derive(velocity_x, 2) + velocity_dx[2])
    stress_yz = stress_yz + time_step * shear_cells * (
        derive(velocity_y, 2) + derive(velocity_z, 1)
    )
    increment = dilation * (stress_xx + stress_yy + stress_zz)
    fields = (
        velocity_x,
        velocity_y,
        velocity_z,
        stress_xx,
        stress_yy,
        stress_zz,
        stress_xy,
        stress_xz,
        stress_yz,
    )
    return (fields, increment)


def on_device(
    lame_lambda,
    lame_mu,
    buoyancy,
    aperture_row,
    wave_state,
    source_cell,
    wavelet,
    receiver_cell,
    prev_row,
    prev_grad,
):
    cells_x = lame_lambda.shape[0]
    shot_index = lax.axis_index("shot")
    tile_index = lax.axis_index("tile")
    my_row = aperture_row[shot_index]
    blank = (jnp.zeros_like(lame_lambda), jnp.zeros_like(lame_mu), jnp.zeros_like(buoyancy))
    pieces = (
        lax.all_gather(lame_lambda, "shot", axis=0, tiled=True),
        lax.all_gather(lame_mu, "shot", axis=0, tiled=True),
        lax.all_gather(buoyancy, "shot", axis=0, tiled=True),
    )
    offset = my_row * cells_x
    span = pieces[0].shape[0]
    inside = (offset >= 0) & (offset < span)
    begin = jnp.clip(offset, 0, span - cells_x)
    lambda_cells, shear_cells, buoy_cells = tuple(
        (
            jnp.where(inside, lax.dynamic_slice_in_dim(piece, begin, cells_x, 0), former)
            for piece, former in zip(pieces, blank)
        )
    )
    local_cells = cells_x * lame_lambda.shape[1] * lame_lambda.shape[2]
    first_cell = tile_index * local_cells
    source_local = source_cell[0] - first_cell
    receivers_local = receiver_cell[0] - first_cell
    state = wave_state[0]
    fields = tuple((state[index] for index in range(9)))

    def advance(carried, amplitude):
        fields, image_sum = carried
        fields, increment = advance_fields(
            fields, buoy_cells, lambda_cells, shear_cells, source_local, amplitude
        )
        record = sample_at(fields[2], receivers_local)
        record = lax.psum(record, "tile")
        return ((fields, image_sum + increment), record)

    (fields, image_sum), records = lax.scan(advance, (fields, jnp.zeros_like(state[0])), wavelet[0])
    grad_local = prev_grad[0]
    target = prev_row[shot_index]
    copies = cells_x * lax.axis_size("shot") // cells_x
    slot = jnp.arange(cells_x * lax.axis_size("shot"), dtype=jnp.int32) // cells_x
    owner_grad = lax.psum_scatter(
        jnp.where((slot == target)[:, None, None], jnp.tile(grad_local, (copies, 1, 1)), 0.0),
        "shot",
        scatter_dimension=0,
        tiled=True,
    )
    return (jnp.stack(fields)[None], image_sum[None], owner_grad, records[None])


def solution(mesh):
    placed = (
        P(("shot", "tile"), None, None),
        P(("shot", "tile"), None, None),
        P(("shot", "tile"), None, None),
        P(),
        P("shot", None, "tile", None, None),
        P("shot"),
        P("shot", None),
        P("shot", None),
        P(),
        P("shot", "tile", None, None),
    )
    return jax.shard_map(
        on_device,
        mesh=mesh,
        in_specs=placed,
        out_specs=(
            P("shot", None, "tile", None, None),
            P("shot", "tile", None, None),
            P(("shot", "tile"), None, None),
            P("shot", None, None),
        ),
        check_vma=False,
    )
```

profile of v0, /device:TPU:2, one launch (start us, length us, event | category | flops | bytes accessed | tf_op | source)
XLA Modules:
  0.0 699.9 jit_solution(10449325736466602303)
XLA Ops:
  17.0 42.5 %all-gather.4.cloned.1.call-done = f32[64,32,256]{2,1,0:T(8,128)} async-done(((f32[4,32,256]{2,1,0:T(8,128)}), f32[64,32,256]{2,1,0:T(8,128)}) %all-gather.4.cloned.1.call-update) | async-done | bytes 2097168 | tf_op jit(solution)/shard_map/all_gather | solution.py:140
  61.9 46.6 %all-gather.8.cloned.1.call-done = f32[64,32,256]{2,1,0:T(8,128)} async-done(((f32[4,32,256]{2,1,0:T(8,128)}), f32[64,32,256]{2,1,0:T(8,128)}) %all-gather.8.cloned.1.call-update) | async-done | bytes 2097168 | tf_op jit(solution)/shard_map/all_gather | solution.py:139
  109.4 48.0 %all-gather.6.cloned.1.call-done = f32[64,32,256]{2,1,0:T(8,128)} async-done(((f32[4,32,256]{2,1,0:T(8,128)}), f32[64,32,256]{2,1,0:T(8,128)}) %all-gather.6.cloned.1.call-update) | async-done | bytes 2097168 | tf_op jit(solution)/shard_map/all_gather | solution.py:138
  158.4 533.2 %while.34 = (s32[]{:T(128)}, f32[4,32,256]{2,1,0:T(8,128)S(1)}, f32[4,32,256]{2,1,0:T(8,128)S(1)}, f32[4,32,256]{2,1,0:T(8,128)S(1)}, f32[4,32,256]{2,1,0:T(8,12...) while((s32[]{:T(128)}, f32[4,32,256]{2,1,0:T(8,128)S(1)}, ...), condition=%wide.region_2.3_spmd.clone, body=%wide.region_0.2_spmd.clone.sunk | while | flops 10718471 | bytes 27152824 | solution.py:168
  158.4 5.5 collective-permute-start
  167.1 5.6 collective-permute-done
  172.7 6.2 collective-permute-done.1
  182.5 3.9 collective-permute-start.3
  188.2 18.3 %psum.12 = f32[1,256]{1,0:T(1,128)S(1)} all-reduce(f32[1,256]{1,0:T(1,128)S(1)} %bitcast.139), channel_id=1, replica_groups=mesh['shot'=16,'tile'=8] {'tile'}, use_global_device_ids=true, to_apply=%region_1.1 | all-reduce | flops 256 | bytes 2048 | tf_op jit(solution)/shard_map/while/body/eval_jaxpr/psum | solution.py:165
  217.6 6.8 collective-permute-done.1
  228.0 3.9 collective-permute-start.3
  233.8 18.1 %psum.12 = f32[1,256]{1,0:T(1,128)S(1)} all-reduce(f32[1,256]{1,0:T(1,128)S(1)} %bitcast.139), channel_id=1, replica_groups=mesh['shot'=16,'tile'=8] {'tile'}, use_global_device_ids=true, to_apply=%region_1.1 | all-reduce | flops 256 | bytes 2048 | tf_op jit(solution)/shard_map/while/body/eval_jaxpr/psum | solution.py:165
  255.2 3.9 collective-permute-start.1
  263.9 4.0 collective-permute-done.1
  271.5 3.9 collective-permute-start.3
  277.3 18.1 %psum.12 = f32[1,256]{1,0:T(1,128)S(1)} all-reduce(f32[1,256]{1,0:T(1,128)S(1)} %bitcast.139), channel_id=1, replica_groups=mesh['shot'=16,'tile'=8] {'tile'}, use_global_device_ids=true, to_apply=%region_1.1 | all-reduce | flops 256 | bytes 2048 | tf_op jit(solution)/shard_map/while/body/eval_jaxpr/psum | solution.py:165
  298.8 3.9 collective-permute-start.1
  304.0 4.6 collective-permute-done
  308.6 4.1 collective-permute-done.1
  316.2 3.9 collective-permute-start.3
  322.0 18.2 %psum.12 = f32[1,256]{1,0:T(1,128)S(1)} all-reduce(f32[1,256]{1,0:T(1,128)S(1)} %bitcast.139), channel_id=1, replica_groups=mesh['shot'=16,'tile'=8] {'tile'}, use_global_device_ids=true, to_apply=%region_1.1 | all-reduce | flops 256 | bytes 2048 | tf_op jit(solution)/shard_map/while/body/eval_jaxpr/psum | solution.py:165
  343.5 3.9 collective-permute-start.1
  351.3 4.1 collective-permute-done.1
  358.9 3.9 collective-permute-start.3
  364.7 19.1 %psum.12 = f32[1,256]{1,0:T(1,128)S(1)} all-reduce(f32[1,256]{1,0:T(1,128)S(1)} %bitcast.139), channel_id=1, replica_groups=mesh['shot'=16,'tile'=8] {'tile'}, use_global_device_ids=true, to_apply=%region_1.1 | all-reduce | flops 256 | bytes 2048 | tf_op jit(solution)/shard_map/while/body/eval_jaxpr/psum | solution.py:165
  394.9 6.0 collective-permute-done.1
  404.4 3.9 collective-permute-start.3
  410.2 18.2 %psum.12 = f32[1,256]{1,0:T(1,128)S(1)} all-reduce(f32[1,256]{1,0:T(1,128)S(1)} %bitcast.139), channel_id=1, replica_groups=mesh['shot'=16,'tile'=8] {'tile'}, use_global_device_ids=true, to_apply=%region_1.1 | all-reduce | flops 256 | bytes 2048 | tf_op jit(solution)/shard_map/while/body/eval_jaxpr/psum | solution.py:165
  431.7 3.9 collective-permute-start.1
  439.5 4.0 collective-permute-done.1
  447.1 3.9 collective-permute-start.3
  452.8 18.2 %psum.12 = f32[1,256]{1,0:T(1,128)S(1)} all-reduce(f32[1,256]{1,0:T(1,128)S(1)} %bitcast.139), channel_id=1, replica_groups=mesh['shot'=16,'tile'=8] {'tile'}, use_global_device_ids=true, to_apply=%region_1.1 | all-reduce | flops 256 | bytes 2048 | tf_op jit(solution)/shard_map/while/body/eval_jaxpr/psum | solution.py:165
  474.4 3.9 collective-permute-start.1
  479.6 3.9 collective-permute-done
  483.5 4.0 collective-permute-done.1
  496.8 18.1 %psum.12 = f32[1,256]{1,0:T(1,128)S(1)} all-reduce(f32[1,256]{1,0:T(1,128)S(1)} %bitcast.139), channel_id=1, replica_groups=mesh['shot'=16,'tile'=8] {'tile'}, use_global_device_ids=true, to_apply=%region_1.1 | all-reduce | flops 256 | bytes 2048 | tf_op jit(solution)/shard_map/while/body/eval_jaxpr/psum | solution.py:165
  523.5 4.5 collective-permute-done
  528.0 5.8 collective-permute-done.1
  537.3 3.9 collective-permute-start.3
  543.1 18.1 %psum.12 = f32[1,256]{1,0:T(1,128)S(1)} all-reduce(f32[1,256]{1,0:T(1,128)S(1)} %bitcast.139), channel_id=1, replica_groups=mesh['shot'=16,'tile'=8] {'tile'}, use_global_device_ids=true, to_apply=%region_1.1 | all-reduce | flops 256 | bytes 2048 | tf_op jit(solution)/shard_map/while/body/eval_jaxpr/psum | solution.py:165
  572.3 4.4 collective-permute-done.1
  586.0 18.1 %psum.12 = f32[1,256]{1,0:T(1,128)S(1)} all-reduce(f32[1,256]{1,0:T(1,128)S(1)} %bitcast.139), channel_id=1, replica_groups=mesh['shot'=16,'tile'=8] {'tile'}, use_global_device_ids=true, to_apply=%region_1.1 | all-reduce | flops 256 | bytes 2048 | tf_op jit(solution)/shard_map/while/body/eval_jaxpr/psum | solution.py:165
  616.1 4.0 collective-permute-done.1
  629.5 18.1 %psum.12 = f32[1,256]{1,0:T(1,128)S(1)} all-reduce(f32[1,256]{1,0:T(1,128)S(1)} %bitcast.139), channel_id=1, replica_groups=mesh['shot'=16,'tile'=8] {'tile'}, use_global_device_ids=true, to_apply=%region_1.1 | all-reduce | flops 256 | bytes 2048 | tf_op jit(solution)/shard_map/while/body/eval_jaxpr/psum | solution.py:165
  651.0 3.9 collective-permute-start.1
  658.7 4.0 collective-permute-done.1
  666.3 3.9 collective-permute-start.3
  672.0 18.1 %psum.12 = f32[1,256]{1,0:T(1,128)S(1)} all-reduce(f32[1,256]{1,0:T(1,128)S(1)} %bitcast.139), channel_id=1, replica_groups=mesh['shot'=16,'tile'=8] {'tile'}, use_global_device_ids=true, to_apply=%region_1.1 | all-reduce | flops 256 | bytes 2048 | tf_op jit(solution)/shard_map/while/body/eval_jaxpr/psum | solution.py:165
  (348 shorter events, 178.0 us)
Async XLA Ops:
  7.2 52.4 %all-gather.4.cloned.1.call-start = ((), (), s32[]{:S(2)}) async-start(), calls=%async_computation.1 | async-start | bytes 2228224 | tf_op jit(solution)/shard_map/all_gather | solution.py:140
  7.9 100.6 %all-gather.8.cloned.1.call-start = ((), (), s32[]{:S(2)}) async-start(), calls=%async_computation.3 | async-start | bytes 2228224 | tf_op jit(solution)/shard_map/all_gather | solution.py:139
  8.6 148.8 %all-gather.6.cloned.1.call-start = ((), (), s32[]{:S(2)}) async-start(), calls=%async_computation.2 | async-start | bytes 2228224 | tf_op jit(solution)/shard_map/all_gather | solution.py:138
  9.4 683.0 %reduce-scatter.2.cloned.1.call-start = ((), (), s32[]{:S(2)}) async-start(), calls=%async_computation.4 | async-start | bytes 2228224 | tf_op jit(solution)/shard_map/reduce_scatter | solution.py:173
  158.4 14.3 %collective-permute-start = (f32[3,4,32,256]{3,2,1,0:T(8,128)S(1)}, f32[3,4,32,256]{3,2,1,0:T(8,128)S(1)}, u32[]{:S(2)}, u32[]{:S(2)}) collective-permute-start(f32[3,4,32,256]{3,2,1,0:T(8,128)S(1)} %pad_maximum_fusion.8), channel_id=1, source_target_pairs={{1,0},{2,1},{3,2},{4,3},{5,4},{6,5},{7,6},{9,8},{10,9},{11,10},{12... | collective-permute-start | bytes 1179656 | tf_op jit(solution)/shard_map/while/body/eval_jaxpr/ppermute | solution.py:20
  164.0 15.0 %collective-permute-start.1 = (f32[3,4,32,256]{3,2,1,0:T(8,128)S(1)}, f32[3,4,32,256]{3,2,1,0:T(8,128)S(1)}, u32[]{:S(2)}, u32[]{:S(2)}) collective-permute-start(f32[3,4,32,256]{3,2,1,0:T(8,128)S(1)} %pad_maximum_fusion.8), channel_id=1, source_target_pairs={{0,1},{1,2},{2,3},{3,4},{4,5},{5,6},{6,7},{8,9},{9,10},{10,11},{11... | collective-permute-start | bytes 1179656 | tf_op jit(solution)/shard_map/while/body/eval_jaxpr/ppermute | solution.py:18
  180.5 26.0 %collective-permute-start.2 = (f32[3,4,32,256]{3,2,1,0:T(8,128)S(1)}, f32[3,4,32,256]{3,2,1,0:T(8,128)S(1)}, u32[]{:S(2)}, u32[]{:S(2)}) collective-permute-start(f32[3,4,32,256]{3,2,1,0:T(8,128)S(1)} %pad_maximum_fusion.10), channel_id=1, source_target_pairs={{1,0},{2,1},{3,2},{4,3},{5,4},{6,5},{7,6},{9,8},{10,9},{11,10},{12... | collective-permute-start | bytes 1179656 | tf_op jit(solution)/shard_map/while/body/eval_jaxpr/ppermute | solution.py:20
  182.5 24.1 %collective-permute-start.3 = (f32[3,4,32,256]{3,2,1,0:T(8,128)S(1)}, f32[3,4,32,256]{3,2,1,0:T(8,128)S(1)}, u32[]{:S(2)}, u32[]{:S(2)}) collective-permute-start(f32[3,4,32,256]{3,2,1,0:T(8,128)S(1)} %pad_maximum_fusion.10), channel_id=1, source_target_pairs={{0,1},{1,2},{2,3},{3,4},{4,5},{5,6},{6,7},{8,9},{9,10},{10,11},{11... | collective-permute-start | bytes 1179656 | tf_op jit(solution)/shard_map/while/body/eval_jaxpr/ppermute | solution.py:18
  211.3 13.2 %collective-permute-start.1 = (f32[3,4,32,256]{3,2,1,0:T(8,128)S(1)}, f32[3,4,32,256]{3,2,1,0:T(8,128)S(1)}, u32[]{:S(2)}, u32[]{:S(2)}) collective-permute-start(f32[3,4,32,256]{3,2,1,0:T(8,128)S(1)} %pad_maximum_fusion.8), channel_id=1, source_target_pairs={{0,1},{1,2},{2,3},{3,4},{4,5},{5,6},{6,7},{8,9},{9,10},{10,11},{11... | collective-permute-start | bytes 1179656 | tf_op jit(solution)/shard_map/while/body/eval_jaxpr/ppermute | solution.py:18
  226.1 25.8 %collective-permute-start.2 = (f32[3,4,32,256]{3,2,1,0:T(8,128)S(1)}, f32[3,4,32,256]{3,2,1,0:T(8,128)S(1)}, u32[]{:S(2)}, u32[]{:S(2)}) collective-permute-start(f32[3,4,32,256]{3,2,1,0:T(8,128)S(1)} %pad_maximum_fusion.10), channel_id=1, source_target_pairs={{1,0},{2,1},{3,2},{4,3},{5,4},{6,5},{7,6},{9,8},{10,9},{11,10},{12... | collective-permute-start | bytes 1179656 | tf_op jit(solution)/shard_map/while/body/eval_jaxpr/ppermute | solution.py:20
  228.0 23.9 %collective-permute-start.3 = (f32[3,4,32,256]{3,2,1,0:T(8,128)S(1)}, f32[3,4,32,256]{3,2,1,0:T(8,128)S(1)}, u32[]{:S(2)}, u32[]{:S(2)}) collective-permute-start(f32[3,4,32,256]{3,2,1,0:T(8,128)S(1)} %pad_maximum_fusion.10), channel_id=1, source_target_pairs={{0,1},{1,2},{2,3},{3,4},{4,5},{5,6},{6,7},{8,9},{9,10},{10,11},{11... | collective-permute-start | bytes 1179656 | tf_op jit(solution)/shard_map/while/body/eval_jaxpr/ppermute | solution.py:18
  253.3 10.6 %collective-permute-start = (f32[3,4,32,256]{3,2,1,0:T(8,128)S(1)}, f32[3,4,32,256]{3,2,1,0:T(8,128)S(1)}, u32[]{:S(2)}, u32[]{:S(2)}) collective-permute-start(f32[3,4,32,256]{3,2,1,0:T(8,128)S(1)} %pad_maximum_fusion.8), channel_id=1, source_target_pairs={{1,0},{2,1},{3,2},{4,3},{5,4},{6,5},{7,6},{9,8},{10,9},{11,10},{12... | collective-permute-start | bytes 1179656 | tf_op jit(solution)/shard_map/while/body/eval_jaxpr/ppermute | solution.py:20
  255.2 12.7 %collective-permute-start.1 = (f32[3,4,32,256]{3,2,1,0:T(8,128)S(1)}, f32[3,4,32,256]{3,2,1,0:T(8,128)S(1)}, u32[]{:S(2)}, u32[]{:S(2)}) collective-permute-start(f32[3,4,32,256]{3,2,1,0:T(8,128)S(1)} %pad_maximum_fusion.8), channel_id=1, source_target_pairs={{0,1},{1,2},{2,3},{3,4},{4,5},{5,6},{6,7},{8,9},{9,10},{10,11},{11... | collective-permute-start | bytes 1179656 | tf_op jit(solution)/shard_map/while/body/eval_jaxpr/ppermute | solution.py:18
  269.6 25.8 %collective-permute-start.2 = (f32[3,4,32,256]{3,2,1,0:T(8,128)S(1)}, f32[3,4,32,256]{3,2,1,0:T(8,128)S(1)}, u32[]{:S(2)}, u32[]{:S(2)}) collective-permute-start(f32[3,4,32,256]{3,2,1,0:T(8,128)S(1)} %pad_maximum_fusion.10), channel_id=1, source_target_pairs={{1,0},{2,1},{3,2},{4,3},{5,4},{6,5},{7,6},{9,8},{10,9},{11,10},{12... | collective-permute-start | bytes 1179656 | tf_op jit(solution)/shard_map/while/body/eval_jaxpr/ppermute | solution.py:20
  271.5 23.9 %collective-permute-start.3 = (f32[3,4,32,256]{3,2,1,0:T(8,128)S(1)}, f32[3,4,32,256]{3,2,1,0:T(8,128)S(1)}, u32[]{:S(2)}, u32[]{:S(2)}) collective-permute-start(f32[3,4,32,256]{3,2,1,0:T(8,128)S(1)} %pad_maximum_fusion.10), channel_id=1, source_target_pairs={{0,1},{1,2},{2,3},{3,4},{4,5},{5,6},{6,7},{8,9},{9,10},{10,11},{11... | collective-permute-start | bytes 1179656 | tf_op jit(solution)/shard_map/while/body/eval_jaxpr/ppermute | solution.py:18
  296.8 11.7 %collective-permute-start = (f32[3,4,32,256]{3,2,1,0:T(8,128)S(1)}, f32[3,4,32,256]{3,2,1,0:T(8,128)S(1)}, u32[]{:S(2)}, u32[]{:S(2)}) collective-permute-start(f32[3,4,32,256]{3,2,1,0:T(8,128)S(1)} %pad_maximum_fusion.8), channel_id=1, source_target_pairs={{1,0},{2,1},{3,2},{4,3},{5,4},{6,5},{7,6},{9,8},{10,9},{11,10},{12... | collective-permute-start | bytes 1179656 | tf_op jit(solution)/shard_map/while/body/eval_jaxpr/ppermute | solution.py:20
  298.8 13.9 %collective-permute-start.1 = (f32[3,4,32,256]{3,2,1,0:T(8,128)S(1)}, f32[3,4,32,256]{3,2,1,0:T(8,128)S(1)}, u32[]{:S(2)}, u32[]{:S(2)}) collective-permute-start(f32[3,4,32,256]{3,2,1,0:T(8,128)S(1)} %pad_maximum_fusion.8), channel_id=1, source_target_pairs={{0,1},{1,2},{2,3},{3,4},{4,5},{5,6},{6,7},{8,9},{9,10},{10,11},{11... | collective-permute-start | bytes 1179656 | tf_op jit(solution)/shard_map/while/body/eval_jaxpr/ppermute | solution.py:18
  314.3 25.9 %collective-permute-start.2 = (f32[3,4,32,256]{3,2,1,0:T(8,128)S(1)}, f32[3,4,32,256]{3,2,1,0:T(8,128)S(1)}, u32[]{:S(2)}, u32[]{:S(2)}) collective-permute-start(f32[3,4,32,256]{3,2,1,0:T(8,128)S(1)} %pad_maximum_fusion.10), channel_id=1, source_target_pairs={{1,0},{2,1},{3,2},{4,3},{5,4},{6,5},{7,6},{9,8},{10,9},{11,10},{12... | collective-permute-start | bytes 1179656 | tf_op jit(solution)/shard_map/while/body/eval_jaxpr/ppermute | solution.py:20
  316.2 23.9 %collective-permute-start.3 = (f32[3,4,32,256]{3,2,1,0:T(8,128)S(1)}, f32[3,4,32,256]{3,2,1,0:T(8,128)S(1)}, u32[]{:S(2)}, u32[]{:S(2)}) collective-permute-start(f32[3,4,32,256]{3,2,1,0:T(8,128)S(1)} %pad_maximum_fusion.10), channel_id=1, source_target_pairs={{0,1},{1,2},{2,3},{3,4},{4,5},{5,6},{6,7},{8,9},{9,10},{10,11},{11... | collective-permute-start | bytes 1179656 | tf_op jit(solution)/shard_map/while/body/eval_jaxpr/ppermute | solution.py:18
  341.6 9.7 %collective-permute-start = (f32[3,4,32,256]{3,2,1,0:T(8,128)S(1)}, f32[3,4,32,256]{3,2,1,0:T(8,128)S(1)}, u32[]{:S(2)}, u32[]{:S(2)}) collective-permute-start(f32[3,4,32,256]{3,2,1,0:T(8,128)S(1)} %pad_maximum_fusion.8), channel_id=1, source_target_pairs={{1,0},{2,1},{3,2},{4,3},{5,4},{6,5},{7,6},{9,8},{10,9},{11,10},{12... | collective-permute-start | bytes 1179656 | tf_op jit(solution)/shard_map/while/body/eval_jaxpr/ppermute | solution.py:20
  343.5 11.8 %collective-permute-start.1 = (f32[3,4,32,256]{3,2,1,0:T(8,128)S(1)}, f32[3,4,32,256]{3,2,1,0:T(8,128)S(1)}, u32[]{:S(2)}, u32[]{:S(2)}) collective-permute-start(f32[3,4,32,256]{3,2,1,0:T(8,128)S(1)} %pad_maximum_fusion.8), channel_id=1, source_target_pairs={{0,1},{1,2},{2,3},{3,4},{4,5},{5,6},{6,7},{8,9},{9,10},{10,11},{11... | collective-permute-start | bytes 1179656 | tf_op jit(solution)/shard_map/while/body/eval_jaxpr/ppermute | solution.py:18
  357.0 26.8 %collective-permute-start.2 = (f32[3,4,32,256]{3,2,1,0:T(8,128)S(1)}, f32[3,4,32,256]{3,2,1,0:T(8,128)S(1)}, u32[]{:S(2)}, u32[]{:S(2)}) collective-permute-start(f32[3,4,32,256]{3,2,1,0:T(8,128)S(1)} %pad_maximum_fusion.10), channel_id=1, source_target_pairs={{1,0},{2,1},{3,2},{4,3},{5,4},{6,5},{7,6},{9,8},{10,9},{11,10},{12... | collective-permute-start | bytes 1179656 | tf_op jit(solution)/shard_map/while/body/eval_jaxpr/ppermute | solution.py:20
  358.9 24.9 %collective-permute-start.3 = (f32[3,4,32,256]{3,2,1,0:T(8,128)S(1)}, f32[3,4,32,256]{3,2,1,0:T(8,128)S(1)}, u32[]{:S(2)}, u32[]{:S(2)}) collective-permute-start(f32[3,4,32,256]{3,2,1,0:T(8,128)S(1)} %pad_maximum_fusion.10), channel_id=1, source_target_pairs={{0,1},{1,2},{2,3},{3,4},{4,5},{5,6},{6,7},{8,9},{9,10},{10,11},{11... | collective-permute-start | bytes 1179656 | tf_op jit(solution)/shard_map/while/body/eval_jaxpr/ppermute | solution.py:18
  385.2 9.7 %collective-permute-start = (f32[3,4,32,256]{3,2,1,0:T(8,128)S(1)}, f32[3,4,32,256]{3,2,1,0:T(8,128)S(1)}, u32[]{:S(2)}, u32[]{:S(2)}) collective-permute-start(f32[3,4,32,256]{3,2,1,0:T(8,128)S(1)} %pad_maximum_fusion.8), channel_id=1, source_target_pairs={{1,0},{2,1},{3,2},{4,3},{5,4},{6,5},{7,6},{9,8},{10,9},{11,10},{12... | collective-permute-start | bytes 1179656 | tf_op jit(solution)/shard_map/while/body/eval_jaxpr/ppermute | solution.py:20
  389.1 11.8 %collective-permute-start.1 = (f32[3,4,32,256]{3,2,1,0:T(8,128)S(1)}, f32[3,4,32,256]{3,2,1,0:T(8,128)S(1)}, u32[]{:S(2)}, u32[]{:S(2)}) collective-permute-start(f32[3,4,32,256]{3,2,1,0:T(8,128)S(1)} %pad_maximum_fusion.8), channel_id=1, source_target_pairs={{0,1},{1,2},{2,3},{3,4},{4,5},{5,6},{6,7},{8,9},{9,10},{10,11},{11... | collective-permute-start | bytes 1179656 | tf_op jit(solution)/shard_map/while/body/eval_jaxpr/ppermute | solution.py:18
  402.5 25.9 %collective-permute-start.2 = (f32[3,4,32,256]{3,2,1,0:T(8,128)S(1)}, f32[3,4,32,256]{3,2,1,0:T(8,128)S(1)}, u32[]{:S(2)}, u32[]{:S(2)}) collective-permute-start(f32[3,4,32,256]{3,2,1,0:T(8,128)S(1)} %pad_maximum_fusion.10), channel_id=1, source_target_pairs={{1,0},{2,1},{3,2},{4,3},{5,4},{6,5},{7,6},{9,8},{10,9},{11,10},{12... | collective-permute-start | bytes 1179656 | tf_op jit(solution)/shard_map/while/body/eval_jaxpr/ppermute | solution.py:20
  404.4 23.9 %collective-permute-start.3 = (f32[3,4,32,256]{3,2,1,0:T(8,128)S(1)}, f32[3,4,32,256]{3,2,1,0:T(8,128)S(1)}, u32[]{:S(2)}, u32[]{:S(2)}) collective-permute-start(f32[3,4,32,256]{3,2,1,0:T(8,128)S(1)} %pad_maximum_fusion.10), channel_id=1, source_target_pairs={{0,1},{1,2},{2,3},{3,4},{4,5},{5,6},{6,7},{8,9},{9,10},{10,11},{11... | collective-permute-start | bytes 1179656 | tf_op jit(solution)/shard_map/while/body/eval_jaxpr/ppermute | solution.py:18
  431.7 11.8 %collective-permute-start.1 = (f32[3,4,32,256]{3,2,1,0:T(8,128)S(1)}, f32[3,4,32,256]{3,2,1,0:T(8,128)S(1)}, u32[]{:S(2)}, u32[]{:S(2)}) collective-permute-start(f32[3,4,32,256]{3,2,1,0:T(8,128)S(1)} %pad_maximum_fusion.8), channel_id=1, source_target_pairs={{0,1},{1,2},{2,3},{3,4},{4,5},{5,6},{6,7},{8,9},{9,10},{10,11},{11... | collective-permute-start | bytes 1179656 | tf_op jit(solution)/shard_map/while/body/eval_jaxpr/ppermute | solution.py:18
  445.1 25.9 %collective-permute-start.2 = (f32[3,4,32,256]{3,2,1,0:T(8,128)S(1)}, f32[3,4,32,256]{3,2,1,0:T(8,128)S(1)}, u32[]{:S(2)}, u32[]{:S(2)}) collective-permute-start(f32[3,4,32,256]{3,2,1,0:T(8,128)S(1)} %pad_maximum_fusion.10), channel_id=1, source_target_pairs={{1,0},{2,1},{3,2},{4,3},{5,4},{6,5},{7,6},{9,8},{10,9},{11,10},{12... | collective-permute-start | bytes 1179656 | tf_op jit(solution)/shard_map/while/body/eval_jaxpr/ppermute | solution.py:20
  447.1 23.9 %collective-permute-start.3 = (f32[3,4,32,256]{3,2,1,0:T(8,128)S(1)}, f32[3,4,32,256]{3,2,1,0:T(8,128)S(1)}, u32[]{:S(2)}, u32[]{:S(2)}) collective-permute-start(f32[3,4,32,256]{3,2,1,0:T(8,128)S(1)} %pad_maximum_fusion.10), channel_id=1, source_target_pairs={{0,1},{1,2},{2,3},{3,4},{4,5},{5,6},{6,7},{8,9},{9,10},{10,11},{11... | collective-permute-start | bytes 1179656 | tf_op jit(solution)/shard_map/while/body/eval_jaxpr/ppermute | solution.py:18
  472.4 11.0 %collective-permute-start = (f32[3,4,32,256]{3,2,1,0:T(8,128)S(1)}, f32[3,4,32,256]{3,2,1,0:T(8,128)S(1)}, u32[]{:S(2)}, u32[]{:S(2)}) collective-permute-start(f32[3,4,32,256]{3,2,1,0:T(8,128)S(1)} %pad_maximum_fusion.8), channel_id=1, source_target_pairs={{1,0},{2,1},{3,2},{4,3},{5,4},{6,5},{7,6},{9,8},{10,9},{11,10},{12... | collective-permute-start | bytes 1179656 | tf_op jit(solution)/shard_map/while/body/eval_jaxpr/ppermute | solution.py:20
  474.4 13.2 %collective-permute-start.1 = (f32[3,4,32,256]{3,2,1,0:T(8,128)S(1)}, f32[3,4,32,256]{3,2,1,0:T(8,128)S(1)}, u32[]{:S(2)}, u32[]{:S(2)}) collective-permute-start(f32[3,4,32,256]{3,2,1,0:T(8,128)S(1)} %pad_maximum_fusion.8), channel_id=1, source_target_pairs={{0,1},{1,2},{2,3},{3,4},{4,5},{5,6},{6,7},{8,9},{9,10},{10,11},{11... | collective-permute-start | bytes 1179656 | tf_op jit(solution)/shard_map/while/body/eval_jaxpr/ppermute | solution.py:18
  489.2 25.8 %collective-permute-start.2 = (f32[3,4,32,256]{3,2,1,0:T(8,128)S(1)}, f32[3,4,32,256]{3,2,1,0:T(8,128)S(1)}, u32[]{:S(2)}, u32[]{:S(2)}) collective-permute-start(f32[3,4,32,256]{3,2,1,0:T(8,128)S(1)} %pad_maximum_fusion.10), channel_id=1, source_target_pairs={{1,0},{2,1},{3,2},{4,3},{5,4},{6,5},{7,6},{9,8},{10,9},{11,10},{12... | collective-permute-start | bytes 1179656 | tf_op jit(solution)/shard_map/while/body/eval_jaxpr/ppermute | solution.py:20
  491.1 23.9 %collective-permute-start.3 = (f32[3,4,32,256]{3,2,1,0:T(8,128)S(1)}, f32[3,4,32,256]{3,2,1,0:T(8,128)S(1)}, u32[]{:S(2)}, u32[]{:S(2)}) collective-permute-start(f32[3,4,32,256]{3,2,1,0:T(8,128)S(1)} %pad_maximum_fusion.10), channel_id=1, source_target_pairs={{0,1},{1,2},{2,3},{3,4},{4,5},{5,6},{6,7},{8,9},{9,10},{10,11},{11... | collective-permute-start | bytes 1179656 | tf_op jit(solution)/shard_map/while/body/eval_jaxpr/ppermute | solution.py:18
  516.4 11.6 %collective-permute-start = (f32[3,4,32,256]{3,2,1,0:T(8,128)S(1)}, f32[3,4,32,256]{3,2,1,0:T(8,128)S(1)}, u32[]{:S(2)}, u32[]{:S(2)}) collective-permute-start(f32[3,4,32,256]{3,2,1,0:T(8,128)S(1)} %pad_maximum_fusion.8), channel_id=1, source_target_pairs={{1,0},{2,1},{3,2},{4,3},{5,4},{6,5},{7,6},{9,8},{10,9},{11,10},{12... | collective-permute-start | bytes 1179656 | tf_op jit(solution)/shard_map/while/body/eval_jaxpr/ppermute | solution.py:20
  519.8 13.9 %collective-permute-start.1 = (f32[3,4,32,256]{3,2,1,0:T(8,128)S(1)}, f32[3,4,32,256]{3,2,1,0:T(8,128)S(1)}, u32[]{:S(2)}, u32[]{:S(2)}) collective-permute-start(f32[3,4,32,256]{3,2,1,0:T(8,128)S(1)} %pad_maximum_fusion.8), channel_id=1, source_target_pairs={{0,1},{1,2},{2,3},{3,4},{4,5},{5,6},{6,7},{8,9},{9,10},{10,11},{11... | collective-permute-start | bytes 1179656 | tf_op jit(solution)/shard_map/while/body/eval_jaxpr/ppermute | solution.py:18
  535.4 25.8 %collective-permute-start.2 = (f32[3,4,32,256]{3,2,1,0:T(8,128)S(1)}, f32[3,4,32,256]{3,2,1,0:T(8,128)S(1)}, u32[]{:S(2)}, u32[]{:S(2)}) collective-permute-start(f32[3,4,32,256]{3,2,1,0:T(8,128)S(1)} %pad_maximum_fusion.10), channel_id=1, source_target_pairs={{1,0},{2,1},{3,2},{4,3},{5,4},{6,5},{7,6},{9,8},{10,9},{11,10},{12... | collective-permute-start | bytes 1179656 | tf_op jit(solution)/shard_map/while/body/eval_jaxpr/ppermute | solution.py:20
  537.3 23.9 %collective-permute-start.3 = (f32[3,4,32,256]{3,2,1,0:T(8,128)S(1)}, f32[3,4,32,256]{3,2,1,0:T(8,128)S(1)}, u32[]{:S(2)}, u32[]{:S(2)}) collective-permute-start(f32[3,4,32,256]{3,2,1,0:T(8,128)S(1)} %pad_maximum_fusion.10), channel_id=1, source_target_pairs={{0,1},{1,2},{2,3},{3,4},{4,5},{5,6},{6,7},{8,9},{9,10},{10,11},{11... | collective-permute-start | bytes 1179656 | tf_op jit(solution)/shard_map/while/body/eval_jaxpr/ppermute | solution.py:18
  564.9 11.8 %collective-permute-start.1 = (f32[3,4,32,256]{3,2,1,0:T(8,128)S(1)}, f32[3,4,32,256]{3,2,1,0:T(8,128)S(1)}, u32[]{:S(2)}, u32[]{:S(2)}) collective-permute-start(f32[3,4,32,256]{3,2,1,0:T(8,128)S(1)} %pad_maximum_fusion.8), channel_id=1, source_target_pairs={{0,1},{1,2},{2,3},{3,4},{4,5},{5,6},{6,7},{8,9},{9,10},{10,11},{11... | collective-permute-start | bytes 1179656 | tf_op jit(solution)/shard_map/while/body/eval_jaxpr/ppermute | solution.py:18
  578.3 25.8 %collective-permute-start.2 = (f32[3,4,32,256]{3,2,1,0:T(8,128)S(1)}, f32[3,4,32,256]{3,2,1,0:T(8,128)S(1)}, u32[]{:S(2)}, u32[]{:S(2)}) collective-permute-start(f32[3,4,32,256]{3,2,1,0:T(8,128)S(1)} %pad_maximum_fusion.10), channel_id=1, source_target_pairs={{1,0},{2,1},{3,2},{4,3},{5,4},{6,5},{7,6},{9,8},{10,9},{11,10},{12... | collective-permute-start | bytes 1179656 | tf_op jit(solution)/shard_map/while/body/eval_jaxpr/ppermute | solution.py:20
  580.2 23.9 %collective-permute-start.3 = (f32[3,4,32,256]{3,2,1,0:T(8,128)S(1)}, f32[3,4,32,256]{3,2,1,0:T(8,128)S(1)}, u32[]{:S(2)}, u32[]{:S(2)}) collective-permute-start(f32[3,4,32,256]{3,2,1,0:T(8,128)S(1)} %pad_maximum_fusion.10), channel_id=1, source_target_pairs={{0,1},{1,2},{2,3},{3,4},{4,5},{5,6},{6,7},{8,9},{9,10},{10,11},{11... | collective-permute-start | bytes 1179656 | tf_op jit(solution)/shard_map/while/body/eval_jaxpr/ppermute | solution.py:18
  605.5 10.6 %collective-permute-start = (f32[3,4,32,256]{3,2,1,0:T(8,128)S(1)}, f32[3,4,32,256]{3,2,1,0:T(8,128)S(1)}, u32[]{:S(2)}, u32[]{:S(2)}) collective-permute-start(f32[3,4,32,256]{3,2,1,0:T(8,128)S(1)} %pad_maximum_fusion.8), channel_id=1, source_target_pairs={{1,0},{2,1},{3,2},{4,3},{5,4},{6,5},{7,6},{9,8},{10,9},{11,10},{12... | collective-permute-start | bytes 1179656 | tf_op jit(solution)/shard_map/while/body/eval_jaxpr/ppermute | solution.py:20
  607.4 12.8 %collective-permute-start.1 = (f32[3,4,32,256]{3,2,1,0:T(8,128)S(1)}, f32[3,4,32,256]{3,2,1,0:T(8,128)S(1)}, u32[]{:S(2)}, u32[]{:S(2)}) collective-permute-start(f32[3,4,32,256]{3,2,1,0:T(8,128)S(1)} %pad_maximum_fusion.8), channel_id=1, source_target_pairs={{0,1},{1,2},{2,3},{3,4},{4,5},{5,6},{6,7},{8,9},{9,10},{10,11},{11... | collective-permute-start | bytes 1179656 | tf_op jit(solution)/shard_map/while/body/eval_jaxpr/ppermute | solution.py:18
  621.8 25.8 %collective-permute-start.2 = (f32[3,4,32,256]{3,2,1,0:T(8,128)S(1)}, f32[3,4,32,256]{3,2,1,0:T(8,128)S(1)}, u32[]{:S(2)}, u32[]{:S(2)}) collective-permute-start(f32[3,4,32,256]{3,2,1,0:T(8,128)S(1)} %pad_maximum_fusion.10), channel_id=1, source_target_pairs={{1,0},{2,1},{3,2},{4,3},{5,4},{6,5},{7,6},{9,8},{10,9},{11,10},{12... | collective-permute-start | bytes 1179656 | tf_op jit(solution)/shard_map/while/body/eval_jaxpr/ppermute | solution.py:20
  623.7 23.9 %collective-permute-start.3 = (f32[3,4,32,256]{3,2,1,0:T(8,128)S(1)}, f32[3,4,32,256]{3,2,1,0:T(8,128)S(1)}, u32[]{:S(2)}, u32[]{:S(2)}) collective-permute-start(f32[3,4,32,256]{3,2,1,0:T(8,128)S(1)} %pad_maximum_fusion.10), channel_id=1, source_target_pairs={{0,1},{1,2},{2,3},{3,4},{4,5},{5,6},{6,7},{8,9},{9,10},{10,11},{11... | collective-permute-start | bytes 1179656 | tf_op jit(solution)/shard_map/while/body/eval_jaxpr/ppermute | solution.py:18
  651.0 11.8 %collective-permute-start.1 = (f32[3,4,32,256]{3,2,1,0:T(8,128)S(1)}, f32[3,4,32,256]{3,2,1,0:T(8,128)S(1)}, u32[]{:S(2)}, u32[]{:S(2)}) collective-permute-start(f32[3,4,32,256]{3,2,1,0:T(8,128)S(1)} %pad_maximum_fusion.8), channel_id=1, source_target_pairs={{0,1},{1,2},{2,3},{3,4},{4,5},{5,6},{6,7},{8,9},{9,10},{10,11},{11... | collective-permute-start | bytes 1179656 | tf_op jit(solution)/shard_map/while/body/eval_jaxpr/ppermute | solution.py:18
  664.4 25.8 %collective-permute-start.2 = (f32[3,4,32,256]{3,2,1,0:T(8,128)S(1)}, f32[3,4,32,256]{3,2,1,0:T(8,128)S(1)}, u32[]{:S(2)}, u32[]{:S(2)}) collective-permute-start(f32[3,4,32,256]{3,2,1,0:T(8,128)S(1)} %pad_maximum_fusion.10), channel_id=1, source_target_pairs={{1,0},{2,1},{3,2},{4,3},{5,4},{6,5},{7,6},{9,8},{10,9},{11,10},{12... | collective-permute-start | bytes 1179656 | tf_op jit(solution)/shard_map/while/body/eval_jaxpr/ppermute | solution.py:20
  666.3 23.9 %collective-permute-start.3 = (f32[3,4,32,256]{3,2,1,0:T(8,128)S(1)}, f32[3,4,32,256]{3,2,1,0:T(8,128)S(1)}, u32[]{:S(2)}, u32[]{:S(2)}) collective-permute-start(f32[3,4,32,256]{3,2,1,0:T(8,128)S(1)} %pad_maximum_fusion.10), channel_id=1, source_target_pairs={{0,1},{1,2},{2,3},{3,4},{4,5},{5,6},{6,7},{8,9},{9,10},{10,11},{11... | collective-permute-start | bytes 1179656 | tf_op jit(solution)/shard_map/while/body/eval_jaxpr/ppermute | solution.py:18
  (10 other events, 186.4 us)
Sparse Core Ops, SparseCore 0:
  10.4 49.0 all-gather.3
  62.0 46.4 all-gather.7
  111.0 46.4 all-gather.5
  161.7 70.1 reduce-scatter.1
where the time goes:
time: 702 us; the launch traced here: 700 us
  waiting for transfers between devices  238 us (34%)
  blocking collectives  218 us (31%)
  starting transfers between devices  142 us (20%)
  other arithmetic  40.5 us (6%)
  local copies, waits for them, and re-layouts  35.3 us (5%)
  between operations  16 us (2%)
  loops' own time  10 us (1%)
    psum x12, blocking collectives, advance(): record = lax.psum(record, 'tile')  218 us
    ppermute x24, starting transfers between devices, extended(): lax.ppermute(tail, axis, [(i, (i + 1) % count) for i in range(ends)])  87 us
    ppermute x24, waiting for transfers between devices, extended(): lax.ppermute(tail, axis, [(i, (i + 1) % count) for i in range(ends)])  57.5 us
    ppermute x24, starting transfers between devices, extended(): lax.ppermute(head, axis, [((i + 1) % count, i) for i in range(ends)])  54.9 us
    all_gather x1, waiting for transfers between devices, on_device(): lax.all_gather(lame_lambda, 'shot', axis=0, tiled=True)  48 us
    all_gather x1, waiting for transfers between devices, on_device(): lax.all_gather(lame_mu, 'shot', axis=0, tiled=True)  46.6 us
    all_gather x1, waiting for transfers between devices, on_device(): lax.all_gather(buoyancy, 'shot', axis=0, tiled=True)  42.5 us
    ppermute x24, waiting for transfers between devices, extended(): lax.ppermute(head, axis, [((i + 1) % count, i) for i in range(ends)])  41.1 us
  transfers between devices with their start and end apart: 52, of which 27 were waited for; matrix products, arithmetic and copies ran while one was open for 11% of the time, Pallas kernels for 0%

commit v1 on v0

v1 whole, which is shorter than its diff:
```python
import jax
import jax.numpy as jnp
import numpy as np
from jax import lax
from jax.experimental import pallas as pl
from jax.experimental.pallas import tpu as pltpu
from jax.sharding import PartitionSpec as P

MESH = pl.DeviceIdType.MESH
F32 = jnp.float32
BF16 = jnp.bfloat16

WEIGHTS = (672.0, -168.0, 32.0, -3.0)
UNIT = 1.0 / 840.0
DT = 0.2
STEPS = 12

STRESS = (5, 7, 8, 3, 4, 6)
SZZ, SXZ, SYZ, SXX, SYY, SXY = range(6)


def operators():
    gain = np.zeros(9)
    for k in range(1, 5):
        gain[4 + k] = WEIGHTS[k - 1]
        gain[4 - k] = -WEIGHTS[k - 1]

    def at(diff):
        return np.where(np.abs(diff) <= 4, gain[np.clip(diff, -4, 4) + 4], 0.0)

    lane = np.arange(128)
    x, y = lane // 32, lane % 32
    dx = x[:, None] - x[None, :]
    dy = y[:, None] - y[None, :]
    same_y = (dy == 0).astype(np.float64)
    same_x = (dx == 0).astype(np.float64)
    block = np.concatenate(
        [at(dx) * same_y, at(dx - 4) * same_y, at(dx + 4) * same_y, at(dy) * same_x], axis=1
    )
    return np.concatenate([block, block], axis=0)


def split(rows):
    hi = rows.astype(BF16)
    lo = (rows - hi.astype(F32)).astype(BF16)
    return jnp.concatenate([hi, lo], axis=1)


def kernel(
    ap_row, pr_row, wave, lam, mu, buoy, grad, params, weights,
    o_state, o_image, o_owner, o_trace,
    T, RW, TM, G, M, RM, GG, MO, PR, PRO,
    S, V, B, L, MU, MU2, SRC, IMG, R1, L2, TRB, TRS, TRR, OB, D2,
    w_send, w_recv, m_send, m_recv, n_send, n_recv, g_send, g_recv, h_send, h_recv,
    p_send, p_recv, halo_send, halo_recv, vb_send, vb_recv, t_send, t_recv, o_send, o_recv,
):
    s_i = lax.axis_index("shot")
    t_i = lax.axis_index("tile")
    core = s_i % 2
    base = s_i - core
    x_lo = t_i // 4
    y_i = t_i % 4
    role = base + x_lo
    d = 2 * y_i + core
    piece_d = s_i // 2
    half = s_i % 2
    swapped = core != x_lo
    not_self3 = piece_d != d

    barrier = pltpu.get_barrier_semaphore()

    def hello(shot, tile):
        pl.semaphore_signal(barrier, inc=1, device_id=(shot, tile), device_id_type=MESH)

    @pl.when(d == 0)
    def _():
        for par in range(2):
            S[par, :, 0:8] = jnp.zeros((6, 8, 8, 128), F32)
        V[:, 0:4] = jnp.zeros((3, 4, 8, 128), F32)
        B[0:4] = jnp.zeros((4, 8, 128), F32)

    @pl.when(d == 7)
    def _():
        for par in range(2):
            S[par, :, 40:48] = jnp.zeros((6, 8, 8, 128), F32)
        V[:, 36:40] = jnp.zeros((3, 4, 8, 128), F32)
        B[36:40] = jnp.zeros((4, 8, 128), F32)

    for k in range(1, 16):
        hello((s_i + k) % 16, t_i)
    for k in range(1, 8):
        for c in range(2):
            hello(base + c, (t_i + k) % 8)

    @pl.when(not_self3)
    def _():
        hello(2 * d + half, t_i)

    for k in range(8):
        for c in range(2):
            if k == 0 and c == 0:
                continue
            hello(2 * d + (half + c) % 2, (t_i + k) % 8)

    for m, ref in enumerate((lam, mu, buoy)):
        TM[m] = ref[...].T
    for f in range(9):
        T[f] = wave[f].T

    pl.semaphore_wait(barrier, 15 + 14 + 15 + not_self3.astype(jnp.int32))

    def spread_material(k):
        p = (s_i + k) % 16
        return pltpu.make_async_remote_copy(
            src_ref=TM.at[:, pl.ds(16 * p, 16), :],
            dst_ref=G.at[s_i],
            send_sem=m_send.at[k],
            recv_sem=m_recv,
            device_id=(p, t_i),
            device_id_type=MESH,
        )

    spread = [spread_material(k) for k in range(1, 16)]
    for copy in spread:
        copy.start()
    pltpu.make_async_copy(TM.at[:, pl.ds(16 * s_i, 16), :], G.at[s_i], m_recv).start()

    table = pltpu.make_async_remote_copy(
        src_ref=params,
        dst_ref=PRO,
        send_sem=p_send,
        recv_sem=p_recv,
        device_id=(base + 1 - core, t_i),
        device_id_type=MESH,
    )
    table.start()

    def move_wave(k):
        dd = (d + k) % 8
        return pltpu.make_async_remote_copy(
            src_ref=T.at[:, pl.ds(32 * dd, 32), :],
            dst_ref=RW.at[:, pl.ds(32 * t_i, 32), :],
            send_sem=w_send.at[k],
            recv_sem=w_recv,
            device_id=(base + dd % 2, core * 4 + dd // 2),
            device_id_type=MESH,
        )

    waves = [move_wave(k) for k in range(8)]
    for k in range(1, 8):
        waves[k].start()

    @pl.when(swapped)
    def _():
        waves[0].start()

    @pl.when(jnp.logical_not(swapped))
    def _():
        pltpu.make_async_copy(
            T.at[:, pl.ds(32 * d, 32), :], RW.at[:, pl.ds(32 * t_i, 32), :], w_recv
        ).start()

    def spread_grad(k):
        p = (s_i + k) % 16
        return pltpu.make_async_remote_copy(
            src_ref=grad.at[pl.ds(8 * p, 8), :],
            dst_ref=GG.at[s_i],
            send_sem=g_send.at[k],
            recv_sem=g_recv,
            device_id=(p, t_i),
            device_id_type=MESH,
        )

    grads = [spread_grad(k) for k in range(1, 16)]
    for copy in grads:
        copy.start()
    pltpu.make_async_copy(grad.at[pl.ds(8 * s_i, 8), :], GG.at[s_i], g_recv).start()

    pltpu.make_async_copy(G, G, m_recv).wait()
    for s in range(16):
        M[s] = G[ap_row[s]]

    def send_material(k):
        s = (role + k) % 16
        return pltpu.make_async_remote_copy(
            src_ref=M.at[s],
            dst_ref=RM.at[:, pl.ds(32 * t_i + 16 * half, 16), :],
            send_sem=n_send.at[k],
            recv_sem=n_recv,
            device_id=(s - s % 2 + piece_d % 2, (s % 2) * 4 + piece_d // 2),
            device_id_type=MESH,
        )

    deliver = [send_material(k) for k in range(16)]
    for k in range(1, 16):
        deliver[k].start()

    @pl.when(not_self3)
    def _():
        deliver[0].start()

    @pl.when(jnp.logical_not(not_self3))
    def _():
        pltpu.make_async_copy(
            M.at[role], RM.at[:, pl.ds(32 * t_i + 16 * half, 16), :], n_recv
        ).start()

    pltpu.make_async_copy(RW, RW, w_recv).wait()
    for z in range(32):
        for f in range(3):
            V[f, 4 + z] = RW[f, pl.ds(z, 8, stride=32), :]
        for j, f in enumerate(STRESS):
            S[0, j, 8 + z] = RW[f, pl.ds(z, 8, stride=32), :]

    left = jnp.maximum(d - 1, 0)
    right = jnp.minimum(d + 1, 7)
    left_id = (base + left % 2, x_lo * 4 + left // 2)
    right_id = (base + right % 2, x_lo * 4 + right // 2)

    def halo(par):
        def one(side, part, src, dst, device):
            return pltpu.make_async_remote_copy(
                src_ref=src,
                dst_ref=dst,
                send_sem=halo_send.at[par, side, part],
                recv_sem=halo_recv.at[par, side, part],
                device_id=device,
                device_id_type=MESH,
            )

        z3, o3 = pl.ds(0, 3), pl.ds(3, 3)
        to_left = [
            one(0, 0, S.at[par, z3, 8:16], S.at[par, z3, 40:48], left_id),
            one(0, 1, S.at[par, o3, 8:12], S.at[par, o3, 40:44], left_id),
        ]
        to_right = [
            one(1, 0, S.at[par, z3, 32:40], S.at[par, z3, 0:8], right_id),
            one(1, 1, S.at[par, o3, 36:40], S.at[par, o3, 4:8], right_id),
        ]
        return to_left, to_right

    has_left = d > 0
    has_right = d < 7

    def start_halo(par):
        to_left, to_right = halo(par)

        @pl.when(has_left)
        def _():
            for copy in to_left:
                copy.start()

        @pl.when(has_right)
        def _():
            for copy in to_right:
                copy.start()

    def wait_halo(par):
        to_left, to_right = halo(par)

        @pl.when(has_left)
        def _():
            for copy in to_left:
                copy.wait_send()
            for copy in to_right:
                copy.wait_recv()

        @pl.when(has_right)
        def _():
            for copy in to_right:
                copy.wait_send()
            for copy in to_left:
                copy.wait_recv()

    start_halo(0)

    pltpu.make_async_copy(RM, RM, n_recv).wait()
    for z in range(32):
        shear = RM[1, pl.ds(z, 8, stride=32), :] * (DT * UNIT)
        L[z] = RM[0, pl.ds(z, 8, stride=32), :] * (DT * UNIT)
        MU[z] = shear
        MU2[z] = 2.0 * shear
        B[4 + z] = RM[2, pl.ds(z, 8, stride=32), :]

    def vb(side, src_v, dst_v, src_b, dst_b, device):
        return [
            pltpu.make_async_remote_copy(
                src_ref=src, dst_ref=dst, send_sem=vb_send.at[side, i], recv_sem=vb_recv.at[side, i],
                device_id=device, device_id_type=MESH,
            )
            for i, (src, dst) in enumerate(((src_v, dst_v), (src_b, dst_b)))
        ]

    vb_left = vb(0, V.at[:, 4:8], V.at[:, 36:40], B.at[4:8], B.at[36:40], left_id)
    vb_right = vb(1, V.at[:, 32:36], V.at[:, 0:4], B.at[32:36], B.at[0:4], right_id)

    @pl.when(has_left)
    def _():
        for copy in vb_left:
            copy.start()

    @pl.when(has_right)
    def _():
        for copy in vb_right:
            copy.start()

    pltpu.make_async_copy(GG, GG, g_recv).wait()
    for q in range(16):
        total = jnp.zeros((8, 256), F32)
        for s in range(16):
            total = total + jnp.where(pr_row[s] == q, GG[s], 0.0)
        MO[q] = total

    def send_owner(k):
        q = (s_i + k) % 16
        return pltpu.make_async_remote_copy(
            src_ref=MO.at[q],
            dst_ref=o_owner.at[pl.ds(8 * s_i, 8), :],
            send_sem=h_send.at[k],
            recv_sem=h_recv,
            device_id=(q, t_i),
            device_id_type=MESH,
        )

    owners = [send_owner(k) for k in range(1, 16)]
    for copy in owners:
        copy.start()
    pltpu.make_async_copy(MO.at[s_i], o_owner.at[pl.ds(8 * s_i, 8), :], h_recv).start()

    table.wait()

    @pl.when(swapped)
    def _():
        PR[...] = PRO[...]

    @pl.when(jnp.logical_not(swapped))
    def _():
        PR[...] = params[...]

    for part in range(2):
        ids = jnp.broadcast_to(PR[16 + part : 17 + part, :], (128, 128)).T.astype(jnp.int32)
        z = ids & 255
        y = (ids >> 8) & 31
        x = ids >> 13
        mine = (z >> 5) == d
        row = (z & 31) * 8 + (x >> 2)
        lane = (x & 3) * 32 + y
        iota = lax.broadcasted_iota(jnp.int32, (128, 128), 1)
        rows = pl.ds(128 * part, 128)
        for j in range(2):
            hit = jnp.logical_and(mine, row == iota + 128 * j)
            R1[rows, 128 * j : 128 * j + 128] = jnp.where(hit, 1.0, 0.0).astype(BF16)
        here = jnp.where(lane == iota, 1.0, 0.0)
        L2[rows, 0:128] = here
        L2[rows, 128:256] = here

    @pl.when(has_left)
    def _():
        for copy in vb_left:
            copy.wait_send()
        for copy in vb_right:
            copy.wait_recv()

    @pl.when(has_right)
    def _():
        for copy in vb_right:
            copy.wait_send()
        for copy in vb_left:
            copy.wait_recv()

    sub = lax.broadcasted_iota(jnp.int32, (8, 128), 0)
    lane = lax.broadcasted_iota(jnp.int32, (8, 128), 1)
    cell = (4 * sub + lane // 32) * 8192 + (lane % 32) * 256 + (32 * d - 4)
    source = PR[18:19, :].astype(jnp.int32)
    for i in range(40):
        now = B[i]
        SRC[i] = jnp.where(cell + i == source, now * DT, 0.0)
        B[i] = now * (DT * UNIT)
    IMG[...] = jnp.zeros((32, 8, 128), F32)

    first = (sub == 0)[None]
    last = (sub == 7)[None]

    def flat(value):
        return value.reshape(64, 128)

    def along_x(same, before, after):
        down = jnp.where(first, 0.0, pltpu.roll(before.reshape(8, 8, 128), 1, 1))
        up = jnp.where(last, 0.0, pltpu.roll(after.reshape(8, 8, 128), 7, 1))
        return same.reshape(8, 8, 128) + (down + up)

    def along_z(load):
        total = None
        for k in range(1, 5):
            term = WEIGHTS[k - 1] * (load(k) - load(-k))
            total = term if total is None else total + term
        return total

    def velocity(par, i0, amplitude):
        def stress(j, shift=0):
            return S[par, j, pl.ds(i0 + 4 + shift, 8)]

        xs = jnp.concatenate([split(flat(stress(j))) for j in (SXX, SXY, SXZ)], axis=0)
        ys = jnp.concatenate([split(flat(stress(j))) for j in (SYY, SYZ)], axis=0)
        px = jnp.dot(xs, weights[...], preferred_element_type=F32)
        py = jnp.dot(ys, weights[:, 384:512], preferred_element_type=F32)

        def x_of(m):
            rows = px[64 * m : 64 * m + 64]
            return along_x(rows[:, 0:128], rows[:, 128:256], rows[:, 256:384])

        def y_of(rows):
            return rows.reshape(8, 8, 128)

        at = pl.ds(i0, 8)
        gain = B[at]
        V[0, at] = V[0, at] + gain * (
            x_of(0) + y_of(px[64:128, 384:512]) + along_z(lambda k: stress(SXZ, k))
        )
        V[1, at] = V[1, at] + gain * (
            x_of(1) + y_of(py[0:64]) + along_z(lambda k: stress(SYZ, k))
        )
        V[2, at] = (
            V[2, at]
            + gain * (x_of(2) + y_of(py[64:128]) + along_z(lambda k: stress(SZZ, k)))
            + SRC[at] * amplitude
        )

    def stresses(par, z0):
        def speed(j, shift=0):
            return V[j, pl.ds(z0 + 4 + shift, 8)]

        rows = jnp.concatenate([split(flat(speed(j))) for j in range(3)], axis=0)
        p = jnp.dot(rows, weights[...], preferred_element_type=F32)

        def x_of(m):
            r = p[64 * m : 64 * m + 64]
            return along_x(r[:, 0:128], r[:, 128:256], r[:, 256:384])

        def y_of(m):
            return p[64 * m : 64 * m + 64, 384:512].reshape(8, 8, 128)

        old = pl.ds(z0 + 8, 8)
        at = pl.ds(z0, 8)
        other = 1 - par
        shear = MU[at]
        exx = x_of(0)
        eyy = y_of(1)
        ezz = along_z(lambda k: speed(2, k))
        S[other, SXY, old] = S[par, SXY, old] + shear * (y_of(0) + x_of(1))
        S[other, SXZ, old] = S[par, SXZ, old] + shear * (along_z(lambda k: speed(0, k)) + x_of(2))
        S[other, SYZ, old] = S[par, SYZ, old] + shear * (along_z(lambda k: speed(1, k)) + y_of(2))
        div = exx + eyy + ezz
        bulk = L[at] * div
        twice = MU2[at]
        sxx = S[par, SXX, old] + (bulk + twice * exx)
        syy = S[par, SYY, old] + (bulk + twice * eyy)
        szz = S[par, SZZ, old] + (bulk + twice * ezz)
        S[other, SXX, old] = sxx
        S[other, SYY, old] = syy
        S[other, SZZ, old] = szz
        IMG[at] = IMG[at] + div * (sxx + syy + szz)

    def step(n, carry):
        par = lax.rem(n, 2)
        amplitude = PR[pl.ds(n, 1), :]
        for i0 in (8, 16, 24):
            velocity(par, i0, amplitude)
        wait_halo(par)
        for i0 in (0, 32):
            velocity(par, i0, amplitude)
        for z0 in (0, 24):
            stresses(par, z0)

        @pl.when(n < STEPS - 1)
        def _():
            start_halo(1 - par)

        for z0 in (8, 16):
            stresses(par, z0)
        picked = jnp.dot(R1[...], split(V[2, 4:36].reshape(256, 128)), preferred_element_type=F32)
        picked = (picked * L2[...]).astype(BF16)
        TRB[n] = lax.dot_general(
            jnp.ones((8, 256), BF16), picked, (((1,), (1,)), ((), ())), preferred_element_type=F32
        )
        return carry

    lax.fori_loop(0, STEPS, step, 0)

    for n in range(STEPS):
        TRS[n : n + 1, :] = TRB[n, 0:1, :]

    def home(k):
        t = (t_i + k) % 8
        return (base + x_lo, t)

    def send_trace(k):
        return pltpu.make_async_remote_copy(
            src_ref=TRS, dst_ref=TRR.at[d], send_sem=t_send.at[k], recv_sem=t_recv,
            device_id=home(k), device_id_type=MESH,
        )

    def send_home(k):
        t = (t_i + k) % 8
        return pltpu.make_async_remote_copy(
            src_ref=OB.at[:, pl.ds(32 * t, 32), :],
            dst_ref=D2.at[:, pl.ds(32 * d, 32), :],
            send_sem=o_send.at[k],
            recv_sem=o_recv,
            device_id=home(k),
            device_id_type=MESH,
        )

    traces = [send_trace(k) for k in range(8)]
    for k in range(1, 8):
        traces[k].start()

    for z in range(32):
        rows = pl.ds(z, 8, stride=32)
        for f in range(3):
            OB[f, rows, :] = V[f, 4 + z]
        for j, f in enumerate(STRESS):
            OB[f, rows, :] = S[0, j, 8 + z]
        OB[9, rows, :] = IMG[z] * UNIT

    homes = [send_home(k) for k in range(8)]
    for k in range(1, 8):
        homes[k].start()

    @pl.when(swapped)
    def _():
        traces[0].start()
        homes[0].start()

    @pl.when(jnp.logical_not(swapped))
    def _():
        pltpu.make_async_copy(TRS, TRR.at[d], t_recv).start()
        pltpu.make_async_copy(
            OB.at[:, pl.ds(32 * t_i, 32), :], D2.at[:, pl.ds(32 * d, 32), :], o_recv
        ).start()

    for copies in (spread, grads, owners):
        for copy in copies:
            copy.wait_send()
    for k in range(1, 8):
        waves[k].wait_send()
    for k in range(1, 16):
        deliver[k].wait_send()

    @pl.when(swapped)
    def _():
        waves[0].wait_send()

    @pl.when(not_self3)
    def _():
        deliver[0].wait_send()

    pltpu.make_async_copy(o_owner, o_owner, h_recv).wait()

    pltpu.make_async_copy(TRR, TRR, t_recv).wait()
    total = TRR[0]
    for j in range(1, 8):
        total = total + TRR[j]
    o_trace[...] = total

    pltpu.make_async_copy(D2, D2, o_recv).wait()
    for f in range(9):
        o_state[f] = D2[f].T
    o_image[...] = D2[9].T

    for k in range(1, 8):
        traces[k].wait_send()
        homes[k].wait_send()

    @pl.when(swapped)
    def _():
        traces[0].wait_send()
        homes[0].wait_send()


def on_device(
    lame_lambda, lame_mu, buoyancy, aperture_row, wave_state, source_cell, wavelet, receiver_cell,
    prev_row, prev_grad,
):
    rows = jnp.broadcast_to(wavelet[0][:, None], (STEPS, 128))
    params = jnp.concatenate(
        [
            rows,
            jnp.zeros((4, 128), F32),
            receiver_cell[0].reshape(2, 128).astype(F32),
            jnp.broadcast_to(source_cell.astype(F32)[:, None], (1, 128)),
            jnp.zeros((5, 128), F32),
        ],
        axis=0,
    )
    weights = jnp.asarray(operators(), BF16)
    vmem = pl.BlockSpec(memory_space=pltpu.VMEM)
    smem = pl.BlockSpec(memory_space=pltpu.SMEM)
    dma = pltpu.SemaphoreType.DMA
    planes = (8, 128)
    state, image, owner, trace = pl.pallas_call(
        kernel,
        out_shape=(
            jax.ShapeDtypeStruct((9, 128, 256), F32),
            jax.ShapeDtypeStruct((128, 256), F32),
            jax.ShapeDtypeStruct((128, 256), F32),
            jax.ShapeDtypeStruct((STEPS, 256), F32),
        ),
        in_specs=[smem, smem] + [vmem] * 7,
        out_specs=(vmem, vmem, vmem, vmem),
        scratch_shapes=[
            pltpu.VMEM((9, 256, 128), F32),
            pltpu.VMEM((9, 256, 128), F32),
            pltpu.VMEM((3, 256, 128), F32),
            pltpu.VMEM((16, 3, 16, 128), F32),
            pltpu.VMEM((16, 3, 16, 128), F32),
            pltpu.VMEM((3, 256, 128), F32),
            pltpu.VMEM((16, 8, 256), F32),
            pltpu.VMEM((16, 8, 256), F32),
            pltpu.VMEM((24, 128), F32),
            pltpu.VMEM((24, 128), F32),
            pltpu.VMEM((2, 6, 48) + planes, F32),
            pltpu.VMEM((3, 40) + planes, F32),
            pltpu.VMEM((40,) + planes, F32),
            pltpu.VMEM((32,) + planes, F32),
            pltpu.VMEM((32,) + planes, F32),
            pltpu.VMEM((32,) + planes, F32),
            pltpu.VMEM((40,) + planes, F32),
            pltpu.VMEM((32,) + planes, F32),
            pltpu.VMEM((256, 256), BF16),
            pltpu.VMEM((256, 256), F32),
            pltpu.VMEM((STEPS, 8, 256), F32),
            pltpu.VMEM((STEPS, 256), F32),
            pltpu.VMEM((8, STEPS, 256), F32),
            pltpu.VMEM((10, 256, 128), F32),
            pltpu.VMEM((10, 256, 128), F32),
            dma((8,)), dma, dma((16,)), dma, dma((16,)), dma, dma((16,)), dma, dma((16,)), dma,
            dma, dma, dma((2, 2, 2)), dma((2, 2, 2)), dma((2, 2)), dma((2, 2)),
            dma((8,)), dma, dma((8,)), dma,
        ],
        compiler_params=pltpu.CompilerParams(collective_id=0, has_side_effects=True),
        name="wave",
    )(
        aperture_row,
        prev_row,
        wave_state.reshape(9, 128, 256),
        lame_lambda.reshape(128, 256),
        lame_mu.reshape(128, 256),
        buoyancy.reshape(128, 256),
        prev_grad.reshape(128, 256),
        params,
        weights,
    )
    return (
        state.reshape(1, 9, 4, 32, 256),
        image.reshape(1, 4, 32, 256),
        owner.reshape(4, 32, 256),
        trace[None],
    )


def solution(mesh):
    placed = (
        P(("shot", "tile"), None, None),
        P(("shot", "tile"), None, None),
        P(("shot", "tile"), None, None),
        P(),
        P("shot", None, "tile", None, None),
        P("shot"),
        P("shot", None),
        P("shot", None),
        P(),
        P("shot", "tile", None, None),
    )
    return jax.shard_map(
        on_device,
        mesh=mesh,
        in_specs=placed,
        out_specs=(
            P("shot", None, "tile", None, None),
            P("shot", "tile", None, None),
            P(("shot", "tile"), None, None),
            P("shot", None, None),
        ),
        check_vma=False,
    )
```

time: 702 us -> 128 us (0.18)
  the two profiles are of different devices: /device:TPU:2 before, /device:TPU:25 now
where the time goes in v1:
time: 128 us; the launch traced here: 127 us
  Pallas kernels  117 us (91%)
  local copies, waits for them, and re-layouts  8.32 us (6%)
  between operations  1.3 us (1%)
    pallas_call x1, Pallas kernels, on_device(): pl.pallas_call(kernel, out_shape=(jax.ShapeDtypeStruct((9, 128, 256), F32...  117 us
    unnamed x8, local copies, waits for them, and re-layouts  5.1 us

profile of v1, /device:TPU:25, one launch (start us, length us, event | category | flops | bytes accessed | tf_op | source)
XLA Modules:
  0.0 127.4 jit_solution(3532884238536474613)
XLA Ops:
  1.3 0.7 convert_element_type.9
  2.0 0.7 broadcast_in_dim.25
  2.7 2.5 %concatenate.3.params = f32[24,128]{1,0:T(8,128)} concatenate(f32[12,128]{1,0:T(8,128)S(1)} %broadcast_in_dim.25, f32[4,128]{1,0:T(4,128)S(1)} %broadcast_in_dim.26, f32[2,128]{1,0:T(2,128)S(1)} %bitcast.21, f32[1,128]{1,0:T(1,128)S(1)} %broadcast_in_dim.28, f32[5,128]{1,0:T(8,128)S(1)} %broadcast_in_dim.29), dimensions={0} | concatenate | bytes 24576 | tf_op jit(solution)/shard_map/concatenate | solution.py:586
  5.2 117.1 %wave.1 = (f32[9,128,256]{2,1,0:T(8,128)}, f32[128,256]{1,0:T(8,128)}, f32[128,256]{1,0:T(8,128)}, f32[12,256]{1,0:T(8,128)}) custom-call(s32[16]{0:T(128)} %ap_row.1, s32[16]{0:T(128)} %pr_row.1, f32[9,128,256]{2,1,0:T(8,128)} %bitcast.12, f32[128,256]{1,0:T(8,128)} %bitcast.14, f32[128,256]{1,0:T(8,128)} %bitcast.15, f32[128,256]{1,0:T(8,128)} %bitcast.16, ...), custom_call_target="tpu_custom_call" | custom-call | tf_op jit(solution)/shard_map/wave/pallas_call | solution.py:601
  122.3 1.3 %copy.15 = f32[1,12,256]{2,0,1:T(1,128)} copy(f32[1,12,256]{2,1,0:T(8,128)} %bitcast.20) | data formatting | bytes 24576
  123.6 0.0 copy-start.1
  123.6 0.0 copy-start
  123.6 2.5 %copy.20 = f32[1,9,4,32,256]{4,3,2,1,0:T(8,128)} copy(f32[1,9,4,32,256]{4,3,2,1,0:T(8,128)} %bitcast.13) | data formatting | bytes 2359296
  126.1 0.0 copy-done.1
  126.1 0.7 copy.21
  126.7 0.0 copy-done
  126.7 0.7 copy.22
  (3 shorter events, 0.0 us)
Async XLA Ops:
  123.6 2.5 %copy-start.1 = (f32[128,256]{1,0:T(8,128)S(1)}, f32[128,256]{1,0:T(8,128)}, u32[]{:S(2)}) copy-start(f32[128,256]{1,0:T(8,128)} %get-tuple-element.9) | copy-start | bytes 393220
  123.6 3.1 %copy-start = (f32[128,256]{1,0:T(8,128)S(1)}, f32[128,256]{1,0:T(8,128)}, u32[]{:S(2)}) copy-start(f32[128,256]{1,0:T(8,128)} %get-tuple-element.10) | copy-start | bytes 393220

commit v2 on v0

v2 whole, which is shorter than its diff:
```python
import jax
import jax.numpy as jnp
import numpy as np
from jax import lax
from jax.experimental import pallas as pl
from jax.experimental.pallas import tpu as pltpu
from jax.sharding import PartitionSpec as P

MESH = pl.DeviceIdType.MESH
F32 = jnp.float32
BF16 = jnp.bfloat16

WEIGHTS = (672.0, -168.0, 32.0, -3.0)
UNIT = 1.0 / 840.0
DT = 0.2
STEPS = 12

WAVE_ORDER = (4, 3, 5, 2, 6, 1, 7)

VELOCITY = (0, 1, 2)
WITH_Z = (7, 8, 5)
IN_PLANE = (3, 4, 6)


def operators():
    gain = np.zeros(9)
    for k in range(1, 5):
        gain[4 + k] = WEIGHTS[k - 1]
        gain[4 - k] = -WEIGHTS[k - 1]

    def at(diff):
        return np.where(np.abs(diff) <= 4, gain[np.clip(diff, -4, 4) + 4], 0.0)

    lane = np.arange(128)
    x, y = lane // 32, lane % 32
    dx = x[:, None] - x[None, :]
    dy = y[:, None] - y[None, :]
    same_y = (dy == 0).astype(np.float64)
    same_x = (dx == 0).astype(np.float64)
    block = np.concatenate(
        [at(dx) * same_y, at(dx - 4) * same_y, at(dx + 4) * same_y, at(dy) * same_x], axis=1
    )
    return np.concatenate([block, block], axis=0)


def split(rows):
    hi = rows.astype(BF16)
    lo = (rows - hi.astype(F32)).astype(BF16)
    return jnp.concatenate([hi, lo], axis=1)


def kernel(
    ap_row, pr_row, source, wavelet, receivers, wave, lam, mu, buoy, grad, weights,
    o_planes, o_owner, o_trace,
    T, RW, TM, G, M, RM, GG, MO,
    SZ, SO, V, B, L, MU, MU2, SRC, IMG, HR, QB, QR, R1, L2, TRB, TRS, TRR, OB,
    w_send, w_recv, m_send, m_recv, n_send, n_recv, g_send, g_recv, h_send, h_recv,
    halo_send, halo_recv, b_send, b_recv, t_send, t_recv, o_send, o_recv,
):
    s_i = lax.axis_index("shot")
    t_i = lax.axis_index("tile")

    def snake(i):
        return jnp.where(i < 4, i, 11 - i)

    d = snake(t_i)
    piece_d = s_i // 2
    half = s_i % 2
    elsewhere = piece_d != d
    has_left = d > 0
    has_right = d < 7
    left_id = (s_i, snake(jnp.maximum(d - 1, 0)))
    right_id = (s_i, snake(jnp.minimum(d + 1, 7)))

    def remote(src, dst, send, recv, device):
        return pltpu.make_async_remote_copy(
            src_ref=src, dst_ref=dst, send_sem=send, recv_sem=recv, device_id=device, device_id_type=MESH
        )

    barrier = pltpu.get_barrier_semaphore()

    def hello(shot, tile):
        pl.semaphore_signal(barrier, inc=1, device_id=(shot, tile), device_id_type=MESH)

    for k in range(1, 16):
        hello((s_i + k) % 16, t_i)
    for k in range(1, 8):
        hello(s_i, (t_i + k) % 8)

    @pl.when(elsewhere)
    def _():
        hello(2 * d + half, t_i)

    for k in range(8):
        for c in range(2):
            if k + c:
                hello(2 * d + (half + c) % 2, (t_i + k) % 8)

    for m, ref in enumerate((lam, mu, buoy)):
        TM[m] = ref[...].T
    for f in range(9):
        T[f] = wave[f].T

    SZ[:, 0:4] = jnp.zeros((3, 4, 8, 128), F32)
    SZ[:, 36:40] = jnp.zeros((3, 4, 8, 128), F32)

    def blank(side):
        for par in range(2):
            HR[par, side] = jnp.zeros((3, 4, 8, 128), F32)
            QR[par, side] = jnp.zeros((3, 4, 8, 128), F32)
        B[36 * side : 36 * side + 4] = jnp.zeros((4, 8, 128), F32)

    pl.when(jnp.logical_not(has_left))(lambda: blank(0))
    pl.when(jnp.logical_not(has_right))(lambda: blank(1))

    pl.semaphore_wait(barrier, 15 + 7 + 15 + elsewhere.astype(jnp.int32))

    def spread_material(k):
        p = (s_i + k) % 16
        return remote(TM.at[:, pl.ds(16 * p, 16), :], G.at[s_i], m_send.at[k], m_recv, (p, t_i))

    spread = [spread_material(k) for k in range(1, 16)]
    for copy in spread:
        copy.start()
    pltpu.make_async_copy(TM.at[:, pl.ds(16 * s_i, 16), :], G.at[s_i], m_recv).start()

    def move_wave(k):
        dd = (d + k) % 8
        return remote(
            T.at[:, pl.ds(32 * dd, 32), :],
            RW.at[:, pl.ds(32 * t_i, 32), :],
            w_send.at[k],
            w_recv,
            (s_i, snake(dd)),
        )

    waves = [move_wave(k) for k in WAVE_ORDER]
    for copy in waves:
        copy.start()
    pltpu.make_async_copy(T.at[:, pl.ds(32 * d, 32), :], RW.at[:, pl.ds(32 * t_i, 32), :], w_recv).start()

    iota = lax.broadcasted_iota(jnp.int32, (128, 128), 1)
    for part in range(2):
        ids = jnp.broadcast_to(receivers[:, 128 * part : 128 * part + 128], (128, 128)).astype(F32)
        ids = ids.T.astype(jnp.int32)
        z = ids & 255
        y = (ids >> 8) & 31
        x = ids >> 13
        mine = (z >> 5) == d
        row = (z & 31) * 8 + (x >> 2)
        lane = (x & 3) * 32 + y
        rows = pl.ds(128 * part, 128)
        for j in range(2):
            hit = jnp.logical_and(mine, row == iota + 128 * j)
            R1[rows, 128 * j : 128 * j + 128] = jnp.where(hit, 1.0, 0.0).astype(BF16)
        here = jnp.where(lane == iota, 1.0, 0.0)
        L2[rows, 0:128] = here
        L2[rows, 128:256] = here
    IMG[...] = jnp.zeros((32, 8, 128), F32)

    pltpu.make_async_copy(G, G, m_recv).wait()
    for s in range(16):
        M[s] = G[ap_row[s]]

    def send_material(k):
        s = (s_i + k) % 16
        return remote(
            M.at[s],
            RM.at[:, pl.ds(32 * t_i + 16 * half, 16), :],
            n_send.at[k],
            n_recv,
            (s, snake(piece_d)),
        )

    deliver = [send_material(k) for k in range(16)]
    for k in range(1, 16):
        deliver[k].start()

    @pl.when(elsewhere)
    def _():
        deliver[0].start()

    @pl.when(jnp.logical_not(elsewhere))
    def _():
        pltpu.make_async_copy(M.at[s_i], RM.at[:, pl.ds(32 * t_i + 16 * half, 16), :], n_recv).start()

    def spread_grad(k):
        p = (s_i + k) % 16
        return remote(grad.at[pl.ds(8 * p, 8), :], GG.at[s_i], g_send.at[k], g_recv, (p, t_i))

    grads = [spread_grad(k) for k in range(1, 16)]
    for copy in grads:
        copy.start()
    pltpu.make_async_copy(grad.at[pl.ds(8 * s_i, 8), :], GG.at[s_i], g_recv).start()

    pltpu.make_async_copy(RW, RW, w_recv).wait()
    for z in range(32):
        rows = pl.ds(z, 8, stride=32)
        for j, f in enumerate(WITH_Z):
            SZ[j, 4 + z] = RW[f, rows, :]
        for j, f in enumerate(IN_PLANE):
            SO[j, z] = RW[f, rows, :]
        for j, f in enumerate(VELOCITY):
            V[j, 4 + z] = RW[f, rows, :]

    def halo(par, part):
        def one(side, src, dst, device):
            return remote(src, dst, halo_send.at[par, side, part], halo_recv.at[par, side, part], device)

        if part == 0:
            to_left = one(0, SZ.at[:, 4:8], HR.at[par, 1], left_id)
            to_right = one(1, SZ.at[:, 32:36], HR.at[par, 0], right_id)
        else:
            to_left = one(0, QB.at[par, 0], QR.at[par, 1], left_id)
            to_right = one(1, QB.at[par, 1], QR.at[par, 0], right_id)
        return to_left, to_right

    def start_halo(par, part):
        to_left, to_right = halo(par, part)
        pl.when(has_left)(to_left.start)
        pl.when(has_right)(to_right.start)

    def wait_halo(par):
        for part in range(2):
            to_left, to_right = halo(par, part)

            @pl.when(has_left)
            def _():
                to_left.wait_send()
                to_right.wait_recv()

            @pl.when(has_right)
            def _():
                to_right.wait_send()
                to_left.wait_recv()

    start_halo(0, 0)

    pltpu.make_async_copy(RM, RM, n_recv).wait()
    for z in range(32):
        B[4 + z] = RM[2, pl.ds(z, 8, stride=32), :] * (DT * UNIT)

    b_left = remote(B.at[4:8], B.at[36:40], b_send.at[0], b_recv.at[0], left_id)
    b_right = remote(B.at[32:36], B.at[0:4], b_send.at[1], b_recv.at[1], right_id)
    pl.when(has_left)(b_left.start)
    pl.when(has_right)(b_right.start)

    sub = lax.broadcasted_iota(jnp.int32, (8, 128), 0)
    lane = lax.broadcasted_iota(jnp.int32, (8, 128), 1)
    cell = (4 * sub + lane // 32) * 8192 + (lane % 32) * 256 + 32 * d
    where_source = source[0]
    for z in range(32):
        shear = RM[1, pl.ds(z, 8, stride=32), :] * (DT * UNIT)
        L[z] = RM[0, pl.ds(z, 8, stride=32), :] * (DT * UNIT)
        MU[z] = shear
        MU2[z] = 2.0 * shear
        SRC[z] = jnp.where(cell + z == where_source, RM[2, pl.ds(z, 8, stride=32), :] * DT, 0.0)

    first = (sub == 0)[None]
    last = (sub == 7)[None]

    def flat(value):
        return value.reshape(64, 128)

    def along_x(same, before, after):
        down = jnp.where(first, 0.0, pltpu.roll(before.reshape(8, 8, 128), 1, 1))
        up = jnp.where(last, 0.0, pltpu.roll(after.reshape(8, 8, 128), 7, 1))
        return same.reshape(8, 8, 128) + (down + up)

    def along_z(load):
        total = None
        for k in range(1, 5):
            term = WEIGHTS[k - 1] * (load(k) - load(-k))
            total = term if total is None else total + term
        return total

    def velocity(parts, amplitude):
        def take(ref, *index, shift=0):
            got = [ref[index + (pl.ds(z + shift, n),)] for z, n in parts]
            return got[0] if len(got) == 1 else jnp.concatenate(got, axis=0)

        def with_z(j, shift=0):
            return take(SZ, j, shift=4 + shift)

        fields = (take(SO, 0), take(SO, 2), with_z(0), take(SO, 1), with_z(1))
        xs = jnp.concatenate([split(flat(field)) for field in fields[0:3]], axis=0)
        ys = jnp.concatenate([split(flat(field)) for field in fields[3:5]], axis=0)
        px = jnp.dot(xs, weights[...], preferred_element_type=F32)
        py = jnp.dot(ys, weights[:, 384:512], preferred_element_type=F32)

        def x_of(m):
            rows = px[64 * m : 64 * m + 64]
            return along_x(rows[:, 0:128], rows[:, 128:256], rows[:, 256:384])

        def y_of(rows):
            return rows.reshape(8, 8, 128)

        ys = (y_of(px[64:128, 384:512]), y_of(py[0:64]), y_of(py[64:128]))
        gain = take(B, shift=4)
        new = [
            take(V, j, shift=4) + gain * (x_of(j) + ys[j] + along_z(lambda k: with_z(j, k)))
            for j in range(3)
        ]
        new[2] = new[2] + take(SRC) * amplitude
        return new

    def inner_velocity(z0, amplitude):
        new = velocity([(z0, 8)], amplitude)
        for j in range(3):
            V[j, pl.ds(z0 + 4, 8)] = new[j]

    def partial_velocity(par, amplitude):
        new = velocity([(0, 4), (28, 4)], amplitude)
        for j in range(3):
            QB[par, 0, j] = new[j][0:4]
            QB[par, 1, j] = new[j][4:8]

    def complete_velocity(par):
        for j in range(4):
            low = high = None
            for k in range(j + 1, 5):
                term = WEIGHTS[k - 1] * HR[par, 0, :, 4 + j - k]
                low = term if low is None else low + term
            for k in range(4 - j, 5):
                term = WEIGHTS[k - 1] * HR[par, 1, :, j - 4 + k]
                high = term if high is None else high + term
            V[:, 4 + j] = QB[par, 0, :, j] - B[4 + j] * low
            V[:, 32 + j] = QB[par, 1, :, j] + B[32 + j] * high
            low = high = None
            for k in range(4 - j, 5):
                term = WEIGHTS[k - 1] * SZ[:, j + k]
                low = term if low is None else low + term
            for k in range(j + 1, 5):
                term = WEIGHTS[k - 1] * SZ[:, 36 + j - k]
                high = term if high is None else high + term
            V[:, j] = QR[par, 0, :, j] + B[j] * low
            V[:, 36 + j] = QR[par, 1, :, j] - B[36 + j] * high

    def stresses(z0):
        def speed(j, shift=0):
            return V[j, pl.ds(z0 + 4 + shift, 8)]

        rows = jnp.concatenate([split(flat(speed(j))) for j in range(3)], axis=0)
        p = jnp.dot(rows, weights[...], preferred_element_type=F32)

        def x_of(m):
            r = p[64 * m : 64 * m + 64]
            return along_x(r[:, 0:128], r[:, 128:256], r[:, 256:384])

        def y_of(m):
            return p[64 * m : 64 * m + 64, 384:512].reshape(8, 8, 128)

        at = pl.ds(z0, 8)
        wide = pl.ds(z0 + 4, 8)
        shear = MU[at]
        exx = x_of(0)
        eyy = y_of(1)
        ezz = along_z(lambda k: speed(2, k))
        SZ[0, wide] = SZ[0, wide] + shear * (along_z(lambda k: speed(0, k)) + x_of(2))
        SZ[1, wide] = SZ[1, wide] + shear * (along_z(lambda k: speed(1, k)) + y_of(2))
        SO[2, at] = SO[2, at] + shear * (y_of(0) + x_of(1))
        div = exx + eyy + ezz
        bulk = L[at] * div
        twice = MU2[at]
        szz = SZ[2, wide] + (bulk + twice * ezz)
        sxx = SO[0, at] + (bulk + twice * exx)
        syy = SO[1, at] + (bulk + twice * eyy)
        SZ[2, wide] = szz
        SO[0, at] = sxx
        SO[1, at] = syy
        IMG[at] = IMG[at] + div * (sxx + syy + szz)

    def send_owner(k):
        q = (s_i + k) % 16
        return remote(MO.at[q], o_owner.at[pl.ds(8 * s_i, 8), :], h_send.at[k], h_recv, (q, t_i))

    owners = [send_owner(k) for k in range(1, 16)]

    def gradients():
        pltpu.make_async_copy(GG, GG, g_recv).wait()
        for q in range(16):
            total = jnp.zeros((8, 256), F32)
            for s in range(16):
                total = total + jnp.where(pr_row[s] == q, GG[s], 0.0)
            MO[q] = total
        for copy in owners:
            copy.start()
        pltpu.make_async_copy(MO.at[s_i], o_owner.at[pl.ds(8 * s_i, 8), :], h_recv).start()

    partial_velocity(0, wavelet[0, 0])
    start_halo(0, 1)

    @pl.when(has_left)
    def _():
        b_left.wait_send()
        b_right.wait_recv()

    @pl.when(has_right)
    def _():
        b_right.wait_send()
        b_left.wait_recv()

    def step(n, carry):
        par = lax.rem(n, 2)
        amplitude = wavelet[0, n]
        for z0 in (4, 12, 20):
            inner_velocity(z0, amplitude)
        wait_halo(par)
        complete_velocity(par)
        for z0 in (0, 24):
            stresses(z0)

        @pl.when(n < STEPS - 1)
        def _():
            start_halo(1 - par, 0)
            partial_velocity(1 - par, wavelet[0, jnp.minimum(n + 1, STEPS - 1)])
            start_halo(1 - par, 1)

        for z0 in (8, 16):
            stresses(z0)
        picked = jnp.dot(R1[...], split(V[2, 4:36].reshape(256, 128)), preferred_element_type=F32)
        picked = (picked * L2[...]).astype(BF16)
        TRB[n] = lax.dot_general(
            jnp.ones((8, 256), BF16), picked, (((1,), (1,)), ((), ())), preferred_element_type=F32
        )
        pl.when(n == 1)(gradients)
        return carry

    lax.fori_loop(0, STEPS, step, 0)

    for z in range(32):
        rows = pl.ds(z, 8, stride=32)
        for j, f in enumerate(VELOCITY):
            OB[f, rows, :] = V[j, 4 + z]
        for j, f in enumerate(WITH_Z):
            OB[f, rows, :] = SZ[j, 4 + z]
        for j, f in enumerate(IN_PLANE):
            OB[f, rows, :] = SO[j, z]
        OB[9, rows, :] = IMG[z] * UNIT

    def send_home(k):
        t = snake((d + k) % 8)
        return remote(
            OB.at[:, pl.ds(32 * t, 32), :],
            o_planes.at[:, pl.ds(32 * d, 32), :],
            o_send.at[k],
            o_recv,
            (s_i, t),
        )

    homes = [send_home(k) for k in WAVE_ORDER]
    for copy in homes:
        copy.start()
    pltpu.make_async_copy(
        OB.at[:, pl.ds(32 * t_i, 32), :], o_planes.at[:, pl.ds(32 * d, 32), :], o_recv
    ).start()

    for n in range(STEPS):
        TRS[n : n + 1, :] = TRB[n, 0:1, :]

    def send_trace(k):
        return remote(TRS, TRR.at[d], t_send.at[k], t_recv, (s_i, snake((d + k) % 8)))

    traces = [send_trace(k) for k in range(1, 8)]
    for copy in traces:
        copy.start()
    pltpu.make_async_copy(TRS, TRR.at[d], t_recv).start()

    for copies in (spread, grads, owners, waves):
        for copy in copies:
            copy.wait_send()
    for k in range(1, 16):
        deliver[k].wait_send()
    pl.when(elsewhere)(deliver[0].wait_send)
    pltpu.make_async_copy(o_owner, o_owner, h_recv).wait()

    pltpu.make_async_copy(TRR, TRR, t_recv).wait()
    total = TRR[0]
    for j in range(1, 8):
        total = total + TRR[j]
    o_trace[...] = total

    pltpu.make_async_copy(o_planes, o_planes, o_recv).wait()
    for copy in homes + traces:
        copy.wait_send()


def finish(planes, owner, trace, o_state, o_image, o_owner, o_trace):
    for f in range(9):
        o_state[f] = planes[f].T
    o_image[...] = planes[9].T
    o_owner[...] = owner[...]
    o_trace[...] = trace[...]


def on_device(
    lame_lambda, lame_mu, buoyancy, aperture_row, wave_state, source_cell, wavelet, receiver_cell,
    prev_row, prev_grad,
):
    weights = jnp.asarray(operators(), BF16)
    vmem = pl.BlockSpec(memory_space=pltpu.VMEM)
    smem = pl.BlockSpec(memory_space=pltpu.SMEM)
    dma = pltpu.SemaphoreType.DMA
    tile = (8, 128)
    planes, owner, trace = pl.pallas_call(
        kernel,
        out_shape=(
            jax.ShapeDtypeStruct((10, 256, 128), F32),
            jax.ShapeDtypeStruct((128, 256), F32),
            jax.ShapeDtypeStruct((STEPS, 256), F32),
        ),
        in_specs=[smem] * 4 + [vmem] * 7,
        out_specs=(pl.BlockSpec(memory_space=pl.ANY), vmem, vmem),
        scratch_shapes=[
            pltpu.VMEM((9, 256, 128), F32),
            pltpu.VMEM((9, 256, 128), F32),
            pltpu.VMEM((3, 256, 128), F32),
            pltpu.VMEM((16, 3, 16, 128), F32),
            pltpu.VMEM((16, 3, 16, 128), F32),
            pltpu.VMEM((3, 256, 128), F32),
            pltpu.VMEM((16, 8, 256), F32),
            pltpu.VMEM((16, 8, 256), F32),
            pltpu.VMEM((3, 40) + tile, F32),
            pltpu.VMEM((3, 32) + tile, F32),
            pltpu.VMEM((3, 40) + tile, F32),
            pltpu.VMEM((40,) + tile, F32),
            pltpu.VMEM((32,) + tile, F32),
            pltpu.VMEM((32,) + tile, F32),
            pltpu.VMEM((32,) + tile, F32),
            pltpu.VMEM((32,) + tile, F32),
            pltpu.VMEM((32,) + tile, F32),
            pltpu.VMEM((2, 2, 3, 4) + tile, F32),
            pltpu.VMEM((2, 2, 3, 4) + tile, F32),
            pltpu.VMEM((2, 2, 3, 4) + tile, F32),
            pltpu.VMEM((256, 256), BF16),
            pltpu.VMEM((256, 256), F32),
            pltpu.VMEM((STEPS, 8, 256), F32),
            pltpu.VMEM((STEPS, 256), F32),
            pltpu.VMEM((8, STEPS, 256), F32),
            pltpu.VMEM((10, 256, 128), F32),
            dma((8,)), dma, dma((16,)), dma, dma((16,)), dma, dma((16,)), dma, dma((16,)), dma,
            dma((2, 2, 2)), dma((2, 2, 2)), dma((2,)), dma((2,)), dma((8,)), dma, dma((8,)), dma,
        ],
        compiler_params=pltpu.CompilerParams(collective_id=0, has_side_effects=True),
        name="wave",
    )(
        aperture_row,
        prev_row,
        source_cell,
        wavelet,
        receiver_cell,
        wave_state.reshape(9, 128, 256),
        lame_lambda.reshape(128, 256),
        lame_mu.reshape(128, 256),
        buoyancy.reshape(128, 256),
        prev_grad.reshape(128, 256),
        weights,
    )
    state, image, owner, trace = pl.pallas_call(
        finish,
        out_shape=(
            jax.ShapeDtypeStruct((9, 128, 256), F32),
            jax.ShapeDtypeStruct((128, 256), F32),
            jax.ShapeDtypeStruct((128, 256), F32),
            jax.ShapeDtypeStruct((STEPS, 256), F32),
        ),
        in_specs=[vmem] * 3,
        out_specs=(vmem,) * 4,
        name="finish",
    )(planes, owner, trace)
    return (
        state.reshape(1, 9, 4, 32, 256),
        image.reshape(1, 4, 32, 256),
        owner.reshape(4, 32, 256),
        trace[None],
    )


def solution(mesh):
    placed = (
        P(("shot", "tile"), None, None),
        P(("shot", "tile"), None, None),
        P(("shot", "tile"), None, None),
        P(),
        P("shot", None, "tile", None, None),
        P("shot"),
        P("shot", None),
        P("shot", None),
        P(),
        P("shot", "tile", None, None),
    )
    return jax.shard_map(
        on_device,
        mesh=mesh,
        in_specs=placed,
        out_specs=(
            P("shot", None, "tile", None, None),
            P("shot", "tile", None, None),
            P(("shot", "tile"), None, None),
            P("shot", None, None),
        ),
        check_vma=False,
    )
```

time: 702 us -> 127 us (0.18)
  waiting for transfers between devices: 238 us -> 0 us
  blocking collectives: 218 us -> 0 us
  starting transfers between devices: 142 us -> 0 us
  Pallas kernels: 0 us -> 123 us
  other arithmetic: 40.5 us -> 0 us
  local copies, waits for them, and re-layouts: 35.3 us -> 1.33 us
  between operations: 16 us -> 1.29 us
  loops' own time: 10 us -> 0 us
    psum x12 -> x0, blocking collectives: 218 us -> none  [advance(): record = lax.psum(record, 'tile')]
    ppermute x48 -> x0, starting transfers between devices: 142 us -> none  [the longest x24 87 us: extended(): lax.ppermute(tail, axis, [(i, (i + 1) % count) for i in range(ends)])]
    all_gather x3 -> x0, waiting for transfers between devices: 137 us -> none  [the longest x1 48 us: on_device(): lax.all_gather(lame_lambda, 'shot', axis=0, tiled=True)]
    pallas_call x0 -> x2, Pallas kernels: none -> 123 us  [the longest x1 120 us: on_device(): pl.pallas_call(kernel, out_shape=(jax.ShapeDtypeStruct((10, 256, 128), F3...]
    ppermute x48 -> x0, waiting for transfers between devices: 98.6 us -> none  [the longest x24 57.5 us: extended(): lax.ppermute(tail, axis, [(i, (i + 1) % count) for i in range(ends)])]
    add x60 -> x0, other arithmetic: 27.1 us -> none  [the longest x12 10.7 us: advance_fields(): velocity_z + time_step * buoy_cells * (stress_dx[2] + derive(stress_yz, 1...]
    gather x12 -> x0, local copies, waits for them, and re-layouts: 20.7 us -> none  [sample_at(): return jnp.where(inside, flat[index_at], 0.0)]
    another operation x1 -> x0, loops' own time: 10 us -> none  [on_device(): lax.scan(advance, (fields, jnp.zeros_like(state[0])), wavelet[0])]
  transfers between devices with their start and end apart: 52 -> 0, of which waited for: 27 -> 0; matrix products, arithmetic and copies ran while one was open for 11% -> 0% of each run, Pallas kernels for 0% -> 0%
where the time goes in v2:
time: 127 us; the launch traced here: 126 us
  Pallas kernels  123 us (97%)
  local copies, waits for them, and re-layouts  1.33 us (1%)
  between operations  1.29 us (1%)
    pallas_call x1, Pallas kernels, on_device(): pl.pallas_call(kernel, out_shape=(jax.ShapeDtypeStruct((10, 256, 128), F3...  120 us
    pallas_call x1, Pallas kernels, on_device(): pl.pallas_call(finish, out_shape=(jax.ShapeDtypeStruct((9, 128, 256), F32...  2.86 us

profile of v2, /device:TPU:2, one launch (start us, length us, event | category | flops | bytes accessed | tf_op | source)
XLA Modules:
  0.0 125.8 jit_solution(12019516324492520031)
XLA Ops:
  1.3 120.4 %wave.1 = (f32[10,256,128]{2,1,0:T(8,128)}, f32[128,256]{1,0:T(8,128)}, f32[12,256]{1,0:T(8,128)}) custom-call(s32[16]{0:T(128)} %ap_row.1, s32[16]{0:T(128)} %pr_row.1, s32[1]{0:T(128)S(6)} %copy.16.source, f32[1,12]{1,0:T(1,128)} %wavelet.1, s32[1,256]{1,0:T(1,128)} %receivers.1, f32[9,128,256]{2,1,0:T(8,128)} %bitcast.9, f32[128,256]{1,0:T(8,128)} %bitcast.10, ...), custom_call_target="tpu_custom_call" | custom-call | tf_op jit(solution)/shard_map/wave/pallas_call | solution.py:505
  121.7 2.9 %finish.1 = (f32[9,128,256]{2,1,0:T(8,128)}, f32[128,256]{1,0:T(8,128)}, f32[128,256]{1,0:T(8,128)}, f32[12,256]{1,0:T(8,128)}) custom-call(f32[10,256,128]{2,1,0:T(8,128)} %get-tuple-element.11.planes, f32[128,256]{1,0:T(8,128)} %get-tuple-element.12.owner, f32[12,256]{1,0:T(8,128)} %get-tuple-element.13.trace), custom_call_target="tpu_custom_call" | custom-call | tf_op jit(solution)/shard_map/finish/pallas_call | solution.py:559
  124.5 1.3 %copy.15 = f32[1,12,256]{2,0,1:T(1,128)} copy(f32[1,12,256]{2,1,0:T(8,128)} %bitcast.14) | data formatting | bytes 24576

commit v3 on v2

--- a/solution.py
+++ b/solution.py
@@ -15,7 +15,7 @@
 DT = 0.2
 STEPS = 12
 
-WAVE_ORDER = (4, 3, 5, 2, 6, 1, 7)
+WAVE_ORDER = (1, 3, 2, 4, 5, 7, 6)
 
 VELOCITY = (0, 1, 2)
 WITH_Z = (7, 8, 5)
@@ -64,8 +64,9 @@
         return jnp.where(i < 4, i, 11 - i)
 
     d = snake(t_i)
-    piece_d = s_i // 2
-    half = s_i % 2
+    piece = (s_i + 2 * t_i) % 16
+    piece_d = piece // 2
+    half = piece % 2
     elsewhere = piece_d != d
     has_left = d > 0
     has_right = d < 7
@@ -89,12 +90,13 @@
 
     @pl.when(elsewhere)
     def _():
-        hello(2 * d + half, t_i)
+        hello((2 * d + half - 2 * t_i + 16) % 16, t_i)
 
     for k in range(8):
+        tile = (t_i + k) % 8
         for c in range(2):
             if k + c:
-                hello(2 * d + (half + c) % 2, (t_i + k) % 8)
+                hello((2 * d + (half + c) % 2 - 2 * tile + 16) % 16, tile)
 
     for m, ref in enumerate((lam, mu, buoy)):
         TM[m] = ref[...].T
@@ -117,15 +119,17 @@
 
     def spread_material(k):
         p = (s_i + k) % 16
-        return remote(TM.at[:, pl.ds(16 * p, 16), :], G.at[s_i], m_send.at[k], m_recv, (p, t_i))
+        rows = 16 * ((p + 2 * t_i) % 16)
+        return remote(TM.at[:, pl.ds(rows, 16), :], G.at[s_i], m_send.at[k], m_recv, (p, t_i))
 
     spread = [spread_material(k) for k in range(1, 16)]
     for copy in spread:
         copy.start()
-    pltpu.make_async_copy(TM.at[:, pl.ds(16 * s_i, 16), :], G.at[s_i], m_recv).start()
+    pltpu.make_async_copy(TM.at[:, pl.ds(16 * piece, 16), :], G.at[s_i], m_recv).start()
 
     def move_wave(k):
-        dd = (d + k) % 8
+        to = 4 * ((t_i // 4 + k // 4) % 2) + (t_i + k) % 4
+        dd = snake(to)
         return remote(
             T.at[:, pl.ds(32 * dd, 32), :],
             RW.at[:, pl.ds(32 * t_i, 32), :],
@@ -135,8 +139,8 @@
         )
 
     waves = [move_wave(k) for k in WAVE_ORDER]
-    for copy in waves:
-        copy.start()
+    for i in (0, 1, 2, 5, 6):
+        waves[i].start()
     pltpu.make_async_copy(T.at[:, pl.ds(32 * d, 32), :], RW.at[:, pl.ds(32 * t_i, 32), :], w_recv).start()
 
     iota = lax.broadcasted_iota(jnp.int32, (128, 128), 1)
@@ -184,14 +188,8 @@
     def _():
         pltpu.make_async_copy(M.at[s_i], RM.at[:, pl.ds(32 * t_i + 16 * half, 16), :], n_recv).start()
 
-    def spread_grad(k):
-        p = (s_i + k) % 16
-        return remote(grad.at[pl.ds(8 * p, 8), :], GG.at[s_i], g_send.at[k], g_recv, (p, t_i))
-
-    grads = [spread_grad(k) for k in range(1, 16)]
-    for copy in grads:
-        copy.start()
-    pltpu.make_async_copy(grad.at[pl.ds(8 * s_i, 8), :], GG.at[s_i], g_recv).start()
+    for i in (3, 4):
+        waves[i].start()
 
     pltpu.make_async_copy(RW, RW, w_recv).wait()
     for z in range(32):
@@ -370,6 +368,16 @@
         SO[1, at] = syy
         IMG[at] = IMG[at] + div * (sxx + syy + szz)
 
+    def spread_grad(k):
+        p = (s_i + k) % 16
+        return remote(grad.at[pl.ds(8 * p, 8), :], GG.at[s_i], g_send.at[k], g_recv, (p, t_i))
+
+    grads = [spread_grad(k) for k in range(1, 16)]
+    def start_gradients():
+        for copy in grads:
+            copy.start()
+        pltpu.make_async_copy(grad.at[pl.ds(8 * s_i, 8), :], GG.at[s_i], g_recv).start()
+
     def send_owner(k):
         q = (s_i + k) % 16
         return remote(MO.at[q], o_owner.at[pl.ds(8 * s_i, 8), :], h_send.at[k], h_recv, (q, t_i))
@@ -423,7 +431,8 @@
         TRB[n] = lax.dot_general(
             jnp.ones((8, 256), BF16), picked, (((1,), (1,)), ((), ())), preferred_element_type=F32
         )
-        pl.when(n == 1)(gradients)
+        pl.when(n == 1)(start_gradients)
+        pl.when(n == 5)(gradients)
         return carry
 
     lax.fori_loop(0, STEPS, step, 0)
@@ -439,7 +448,7 @@
         OB[9, rows, :] = IMG[z] * UNIT
 
     def send_home(k):
-        t = snake((d + k) % 8)
+        t = 4 * ((t_i // 4 + k // 4) % 2) + (t_i + k) % 4
         return remote(
             OB.at[:, pl.ds(32 * t, 32), :],
             o_planes.at[:, pl.ds(32 * d, 32), :],
@@ -490,7 +499,8 @@
         o_state[f] = planes[f].T
     o_image[...] = planes[9].T
     o_owner[...] = owner[...]
-    o_trace[...] = trace[...]
+    for n in range(STEPS):
+        o_trace[n] = trace[n : n + 1, :]
 
 
 def on_device(
@@ -562,7 +572,7 @@
             jax.ShapeDtypeStruct((9, 128, 256), F32),
             jax.ShapeDtypeStruct((128, 256), F32),
             jax.ShapeDtypeStruct((128, 256), F32),
-            jax.ShapeDtypeStruct((STEPS, 256), F32),
+            jax.ShapeDtypeStruct((STEPS, 1, 256), F32),
         ),
         in_specs=[vmem] * 3,
         out_specs=(vmem,) * 4,
@@ -572,7 +582,7 @@
         state.reshape(1, 9, 4, 32, 256),
         image.reshape(1, 4, 32, 256),
         owner.reshape(4, 32, 256),
-        trace[None],
+        jnp.transpose(trace, (1, 0, 2)),
     )
 
 

time: 127 us -> 114 us (0.90)
  Pallas kernels: 123 us -> 111 us
  local copies, waits for them, and re-layouts: 1.33 us -> 0 us
    pallas_call x1, Pallas kernels: 120 us -> 108 us  [on_device(): pl.pallas_call(kernel, out_shape=(jax.ShapeDtypeStruct((10, 256, 128), F3...]
    unnamed x1 -> x0, local copies, waits for them, and re-layouts: 1.33 us -> none
where the time goes in v3:
time: 114 us; the launch traced here: 113 us
  Pallas kernels  111 us (97%)
  between operations  1.29 us (1%)
    pallas_call x1, Pallas kernels, on_device(): pl.pallas_call(kernel, out_shape=(jax.ShapeDtypeStruct((10, 256, 128), F3...  108 us
    pallas_call x1, Pallas kernels, on_device(): pl.pallas_call(finish, out_shape=(jax.ShapeDtypeStruct((9, 128, 256), F32...  2.86 us

profile of v3, /device:TPU:2, one launch (start us, length us, event | category | flops | bytes accessed | tf_op | source)
XLA Modules:
  0.0 112.6 jit_solution(12202140897113730032)
XLA Ops:
  1.3 108.4 %wave.1 = (f32[10,256,128]{2,1,0:T(8,128)}, f32[128,256]{1,0:T(8,128)}, f32[12,256]{1,0:T(8,128)}) custom-call(s32[16]{0:T(128)} %ap_row.1, s32[16]{0:T(128)} %pr_row.1, s32[1]{0:T(128)S(6)} %copy.15.source, f32[1,12]{1,0:T(1,128)} %wavelet.1, s32[1,256]{1,0:T(1,128)} %receivers.1, f32[9,128,256]{2,1,0:T(8,128)} %bitcast.9, f32[128,256]{1,0:T(8,128)} %bitcast.10, ...), custom_call_target="tpu_custom_call" | custom-call | tf_op jit(solution)/shard_map/wave/pallas_call | solution.py:515
  109.7 2.9 %finish.1 = (f32[9,128,256]{2,1,0:T(8,128)}, f32[128,256]{1,0:T(8,128)}, f32[128,256]{1,0:T(8,128)}, f32[12,1,256]{2,1,0:T(1,128)}) custom-call(f32[10,256,128]{2,1,0:T(8,128)} %get-tuple-element.11.planes, f32[128,256]{1,0:T(8,128)} %get-tuple-element.12.owner, f32[12,256]{1,0:T(8,128)} %get-tuple-element.13.trace), custom_call_target="tpu_custom_call" | custom-call | tf_op jit(solution)/shard_map/finish/pallas_call | solution.py:569

commit v4 on v3

--- a/solution.py
+++ b/solution.py
@@ -50,12 +50,12 @@
 
 
 def kernel(
-    ap_row, pr_row, source, wavelet, receivers, wave, lam, mu, buoy, grad, weights,
+    ap_row, pr_row, source, wavelet, receivers, wave_in, lam_in, mu_in, buoy_in, grad_in, weights_in,
     o_planes, o_owner, o_trace,
-    T, RW, TM, G, M, RM, GG, MO,
-    SZ, SO, V, B, L, MU, MU2, SRC, IMG, HR, QB, QR, R1, L2, TRB, TRS, TRR, OB,
-    w_send, w_recv, m_send, m_recv, n_send, n_recv, g_send, g_recv, h_send, h_recv,
-    halo_send, halo_recv, b_send, b_recv, t_send, t_recv, o_send, o_recv,
+    wave, mats, grad, weights, T, RW, TM, G, M, RM, GG, MO,
+    PRM, PRO, PR, SZ, SO, V, B, L, MU, MU2, SRC, IMG, HR, QB, QR, R1, L2, TRB, TRS, TRR, OB,
+    i_sem, w_send, w_recv, m_send, m_recv, n_send, n_recv, g_send, g_recv, h_send, h_recv,
+    p_send, p_recv, halo_send, halo_recv, b_send, b_recv, t_send, t_recv, o_send, o_recv,
 ):
     s_i = lax.axis_index("shot")
     t_i = lax.axis_index("tile")
@@ -64,20 +64,40 @@
         return jnp.where(i < 4, i, 11 - i)
 
     d = snake(t_i)
+    core = s_i % 2
+    base = s_i - core
+    swapped = d % 2 == 1
+    role = base + (core + d) % 2
     piece = (s_i + 2 * t_i) % 16
     piece_d = piece // 2
     half = piece % 2
     elsewhere = piece_d != d
     has_left = d > 0
     has_right = d < 7
-    left_id = (s_i, snake(jnp.maximum(d - 1, 0)))
-    right_id = (s_i, snake(jnp.minimum(d + 1, 7)))
+    left_id = (base + 1 - core, snake(jnp.maximum(d - 1, 0)))
+    right_id = (base + 1 - core, snake(jnp.minimum(d + 1, 7)))
 
     def remote(src, dst, send, recv, device):
         return pltpu.make_async_remote_copy(
             src_ref=src, dst_ref=dst, send_sem=send, recv_sem=recv, device_id=device, device_id_type=MESH
         )
 
+    loads = [
+        pltpu.make_async_copy(src, dst, i_sem.at[i])
+        for i, (src, dst) in enumerate(
+            (
+                (lam_in, mats.at[0]),
+                (mu_in, mats.at[1]),
+                (buoy_in, mats.at[2]),
+                (wave_in, wave),
+                (grad_in, grad),
+                (weights_in, weights),
+            )
+        )
+    ]
+    for load in loads:
+        load.start()
+
     barrier = pltpu.get_barrier_semaphore()
 
     def hello(shot, tile):
@@ -86,7 +106,8 @@
     for k in range(1, 16):
         hello((s_i + k) % 16, t_i)
     for k in range(1, 8):
-        hello(s_i, (t_i + k) % 8)
+        for c in range(2):
+            hello(base + c, (t_i + k) % 8)
 
     @pl.when(elsewhere)
     def _():
@@ -98,10 +119,20 @@
             if k + c:
                 hello((2 * d + (half + c) % 2 - 2 * tile + 16) % 16, tile)
 
-    for m, ref in enumerate((lam, mu, buoy)):
-        TM[m] = ref[...].T
+    for m in range(3):
+        loads[m].wait()
+        TM[m] = mats[m].T
+    loads[3].wait()
     for f in range(9):
         T[f] = wave[f].T
+    loads[4].wait()
+    loads[5].wait()
+
+    for n in range(STEPS):
+        PRM[n : n + 1, :] = jnp.full((1, 128), wavelet[0, n], F32)
+    for part in range(2):
+        PRM[16 + part : 17 + part, :] = receivers[:, 128 * part : 128 * part + 128].astype(F32)
+    PRM[18:19, :] = jnp.full((1, 128), source[0], jnp.int32).astype(F32)
 
     SZ[:, 0:4] = jnp.zeros((3, 4, 8, 128), F32)
     SZ[:, 36:40] = jnp.zeros((3, 4, 8, 128), F32)
@@ -115,7 +146,7 @@
     pl.when(jnp.logical_not(has_left))(lambda: blank(0))
     pl.when(jnp.logical_not(has_right))(lambda: blank(1))
 
-    pl.semaphore_wait(barrier, 15 + 7 + 15 + elsewhere.astype(jnp.int32))
+    pl.semaphore_wait(barrier, 15 + 14 + 15 + elsewhere.astype(jnp.int32))
 
     def spread_material(k):
         p = (s_i + k) % 16
@@ -126,6 +157,9 @@
     for copy in spread:
         copy.start()
     pltpu.make_async_copy(TM.at[:, pl.ds(16 * piece, 16), :], G.at[s_i], m_recv).start()
+
+    table = remote(PRM, PRO, p_send, p_recv, (base + 1 - core, t_i))
+    table.start()
 
     def move_wave(k):
         to = 4 * ((t_i // 4 + k // 4) % 2) + (t_i + k) % 4
@@ -135,18 +169,44 @@
             RW.at[:, pl.ds(32 * t_i, 32), :],
             w_send.at[k],
             w_recv,
-            (s_i, snake(dd)),
+            (base + (core + dd) % 2, to),
         )
 
     waves = [move_wave(k) for k in WAVE_ORDER]
-    for i in (0, 1, 2, 5, 6):
-        waves[i].start()
-    pltpu.make_async_copy(T.at[:, pl.ds(32 * d, 32), :], RW.at[:, pl.ds(32 * t_i, 32), :], w_recv).start()
+    wave_near = move_wave(0)
+
+    @pl.when(core == 0)
+    def _():
+        for i in (3, 0, 4, 1, 5, 2, 6):
+            waves[i].start()
+
+    @pl.when(core == 1)
+    def _():
+        for i in (0, 1, 2):
+            waves[i].start()
+
+
+    pl.when(swapped)(wave_near.start)
+
+    @pl.when(jnp.logical_not(swapped))
+    def _():
+        pltpu.make_async_copy(
+            T.at[:, pl.ds(32 * d, 32), :], RW.at[:, pl.ds(32 * t_i, 32), :], w_recv
+        ).start()
+
+    table.wait()
+
+    @pl.when(swapped)
+    def _():
+        PR[...] = PRO[...]
+
+    @pl.when(jnp.logical_not(swapped))
+    def _():
+        PR[...] = PRM[...]
 
     iota = lax.broadcasted_iota(jnp.int32, (128, 128), 1)
     for part in range(2):
-        ids = jnp.broadcast_to(receivers[:, 128 * part : 128 * part + 128], (128, 128)).astype(F32)
-        ids = ids.T.astype(jnp.int32)
+        ids = jnp.broadcast_to(PR[16 + part : 17 + part, :], (128, 128)).T.astype(jnp.int32)
         z = ids & 255
         y = (ids >> 8) & 31
         x = ids >> 13
@@ -167,13 +227,13 @@
         M[s] = G[ap_row[s]]
 
     def send_material(k):
-        s = (s_i + k) % 16
+        s = (role + k) % 16
         return remote(
             M.at[s],
             RM.at[:, pl.ds(32 * t_i + 16 * half, 16), :],
             n_send.at[k],
             n_recv,
-            (s, snake(piece_d)),
+            (s - s % 2 + (s % 2 + piece_d) % 2, snake(piece_d)),
         )
 
     deliver = [send_material(k) for k in range(16)]
@@ -186,10 +246,13 @@
 
     @pl.when(jnp.logical_not(elsewhere))
     def _():
-        pltpu.make_async_copy(M.at[s_i], RM.at[:, pl.ds(32 * t_i + 16 * half, 16), :], n_recv).start()
-
-    for i in (3, 4):
-        waves[i].start()
+        pltpu.make_async_copy(M.at[role], RM.at[:, pl.ds(32 * t_i + 16 * half, 16), :], n_recv).start()
+
+
+    @pl.when(core == 1)
+    def _():
+        for i in (3, 4, 5, 6):
+            waves[i].start()
 
     pltpu.make_async_copy(RW, RW, w_recv).wait()
     for z in range(32):
@@ -246,7 +309,7 @@
     sub = lax.broadcasted_iota(jnp.int32, (8, 128), 0)
     lane = lax.broadcasted_iota(jnp.int32, (8, 128), 1)
     cell = (4 * sub + lane // 32) * 8192 + (lane % 32) * 256 + 32 * d
-    where_source = source[0]
+    where_source = PR[18:19, :].astype(jnp.int32)
     for z in range(32):
         shear = RM[1, pl.ds(z, 8, stride=32), :] * (DT * UNIT)
         L[z] = RM[0, pl.ds(z, 8, stride=32), :] * (DT * UNIT)
@@ -395,7 +458,7 @@
             copy.start()
         pltpu.make_async_copy(MO.at[s_i], o_owner.at[pl.ds(8 * s_i, 8), :], h_recv).start()
 
-    partial_velocity(0, wavelet[0, 0])
+    partial_velocity(0, PR[0:1, :])
     start_halo(0, 1)
 
     @pl.when(has_left)
@@ -408,20 +471,53 @@
         b_right.wait_send()
         b_left.wait_recv()
 
+    def send_home(part, k):
+        t = 4 * ((t_i // 4 + k // 4) % 2) + (t_i + k) % 4
+        fields = pl.ds(0, 3) if part == 0 else pl.ds(3, 7)
+        return remote(
+            OB.at[fields, pl.ds(32 * t, 32), :],
+            o_planes.at[fields, pl.ds(32 * d, 32), :],
+            o_send.at[part, k],
+            o_recv,
+            (role, t),
+        )
+
+    homes = [[send_home(part, k) for k in (0,) + WAVE_ORDER] for part in range(2)]
+
+    def start_home(part):
+        for copy in homes[part][1:]:
+            copy.start()
+        pl.when(swapped)(homes[part][0].start)
+        fields = pl.ds(0, 3) if part == 0 else pl.ds(3, 7)
+
+        @pl.when(jnp.logical_not(swapped))
+        def _():
+            pltpu.make_async_copy(
+                OB.at[fields, pl.ds(32 * t_i, 32), :], o_planes.at[fields, pl.ds(32 * d, 32), :], o_recv
+            ).start()
+
+    def velocities_home():
+        for z in range(32):
+            rows = pl.ds(z, 8, stride=32)
+            for j, f in enumerate(VELOCITY):
+                OB[f, rows, :] = V[j, 4 + z]
+        start_home(0)
+
     def step(n, carry):
         par = lax.rem(n, 2)
-        amplitude = wavelet[0, n]
+        amplitude = PR[pl.ds(n, 1), :]
         for z0 in (4, 12, 20):
             inner_velocity(z0, amplitude)
         wait_halo(par)
         complete_velocity(par)
+        pl.when(n == STEPS - 1)(velocities_home)
         for z0 in (0, 24):
             stresses(z0)
 
         @pl.when(n < STEPS - 1)
         def _():
             start_halo(1 - par, 0)
-            partial_velocity(1 - par, wavelet[0, jnp.minimum(n + 1, STEPS - 1)])
+            partial_velocity(1 - par, PR[pl.ds(n + 1, 1), :])
             start_halo(1 - par, 1)
 
         for z0 in (8, 16):
@@ -439,45 +535,32 @@
 
     for z in range(32):
         rows = pl.ds(z, 8, stride=32)
-        for j, f in enumerate(VELOCITY):
-            OB[f, rows, :] = V[j, 4 + z]
         for j, f in enumerate(WITH_Z):
             OB[f, rows, :] = SZ[j, 4 + z]
         for j, f in enumerate(IN_PLANE):
             OB[f, rows, :] = SO[j, z]
         OB[9, rows, :] = IMG[z] * UNIT
-
-    def send_home(k):
-        t = 4 * ((t_i // 4 + k // 4) % 2) + (t_i + k) % 4
-        return remote(
-            OB.at[:, pl.ds(32 * t, 32), :],
-            o_planes.at[:, pl.ds(32 * d, 32), :],
-            o_send.at[k],
-            o_recv,
-            (s_i, t),
-        )
-
-    homes = [send_home(k) for k in WAVE_ORDER]
-    for copy in homes:
-        copy.start()
-    pltpu.make_async_copy(
-        OB.at[:, pl.ds(32 * t_i, 32), :], o_planes.at[:, pl.ds(32 * d, 32), :], o_recv
-    ).start()
+    start_home(1)
 
     for n in range(STEPS):
         TRS[n : n + 1, :] = TRB[n, 0:1, :]
 
     def send_trace(k):
-        return remote(TRS, TRR.at[d], t_send.at[k], t_recv, (s_i, snake((d + k) % 8)))
-
-    traces = [send_trace(k) for k in range(1, 8)]
-    for copy in traces:
+        return remote(TRS, TRR.at[d], t_send.at[k], t_recv, (role, (t_i + k) % 8))
+
+    traces = [send_trace(k) for k in range(8)]
+    for copy in traces[1:]:
         copy.start()
-    pltpu.make_async_copy(TRS, TRR.at[d], t_recv).start()
+    pl.when(swapped)(traces[0].start)
+
+    @pl.when(jnp.logical_not(swapped))
+    def _():
+        pltpu.make_async_copy(TRS, TRR.at[d], t_recv).start()
 
     for copies in (spread, grads, owners, waves):
         for copy in copies:
             copy.wait_send()
+    pl.when(swapped)(wave_near.wait_send)
     for k in range(1, 16):
         deliver[k].wait_send()
     pl.when(elsewhere)(deliver[0].wait_send)
@@ -490,8 +573,13 @@
     o_trace[...] = total
 
     pltpu.make_async_copy(o_planes, o_planes, o_recv).wait()
-    for copy in homes + traces:
+    for copy in homes[0][1:] + homes[1][1:] + traces[1:]:
         copy.wait_send()
+
+    @pl.when(swapped)
+    def _():
+        for copy in (homes[0][0], homes[1][0], traces[0]):
+            copy.wait_send()
 
 
 def finish(planes, owner, trace, o_state, o_image, o_owner, o_trace):
@@ -519,9 +607,13 @@
             jax.ShapeDtypeStruct((128, 256), F32),
             jax.ShapeDtypeStruct((STEPS, 256), F32),
         ),
-        in_specs=[smem] * 4 + [vmem] * 7,
+        in_specs=[smem] * 4 + [vmem] + [pl.BlockSpec(memory_space=pl.ANY)] * 6,
         out_specs=(pl.BlockSpec(memory_space=pl.ANY), vmem, vmem),
         scratch_shapes=[
+            pltpu.VMEM((9, 128, 256), F32),
+            pltpu.VMEM((3, 128, 256), F32),
+            pltpu.VMEM((128, 256), F32),
+            pltpu.VMEM((256, 512), BF16),
             pltpu.VMEM((9, 256, 128), F32),
             pltpu.VMEM((9, 256, 128), F32),
             pltpu.VMEM((3, 256, 128), F32),
@@ -530,6 +622,9 @@
             pltpu.VMEM((3, 256, 128), F32),
             pltpu.VMEM((16, 8, 256), F32),
             pltpu.VMEM((16, 8, 256), F32),
+            pltpu.VMEM((24, 128), F32),
+            pltpu.VMEM((24, 128), F32),
+            pltpu.VMEM((24, 128), F32),
             pltpu.VMEM((3, 40) + tile, F32),
             pltpu.VMEM((3, 32) + tile, F32),
             pltpu.VMEM((3, 40) + tile, F32),
@@ -548,8 +643,8 @@
             pltpu.VMEM((STEPS, 256), F32),
             pltpu.VMEM((8, STEPS, 256), F32),
             pltpu.VMEM((10, 256, 128), F32),
-            dma((8,)), dma, dma((16,)), dma, dma((16,)), dma, dma((16,)), dma, dma((16,)), dma,
-            dma((2, 2, 2)), dma((2, 2, 2)), dma((2,)), dma((2,)), dma((8,)), dma, dma((8,)), dma,
+            dma((6,)), dma((8,)), dma, dma((16,)), dma, dma((16,)), dma, dma((16,)), dma, dma((16,)), dma,
+            dma, dma, dma((2, 2, 2)), dma((2, 2, 2)), dma((2,)), dma((2,)), dma((8,)), dma, dma((2, 8)), dma,
         ],
         compiler_params=pltpu.CompilerParams(collective_id=0, has_side_effects=True),
         name="wave",

time: 114 us -> 111 us (0.974)
  Pallas kernels: 111 us -> 108 us
    pallas_call x1, Pallas kernels: 108 us -> 105 us  [on_device(): pl.pallas_call(kernel, out_shape=(jax.ShapeDtypeStruct((10, 256, 128), F3...]
where the time goes in v4:
time: 111 us; the launch traced here: 109 us
  Pallas kernels  108 us (97%)
  between operations  1.29 us (1%)
    pallas_call x1, Pallas kernels, on_device(): pl.pallas_call(kernel, out_shape=(jax.ShapeDtypeStruct((10, 256, 128), F3...  105 us
    pallas_call x1, Pallas kernels, on_device(): pl.pallas_call(finish, out_shape=(jax.ShapeDtypeStruct((9, 128, 256), F32...  2.86 us

profile of v4, /device:TPU:2, one launch (start us, length us, event | category | flops | bytes accessed | tf_op | source)
XLA Modules:
  0.0 109.1 jit_solution(6541056467196293509)
XLA Ops:
  1.3 104.9 %wave.1 = (f32[10,256,128]{2,1,0:T(8,128)}, f32[128,256]{1,0:T(8,128)}, f32[12,256]{1,0:T(8,128)}) custom-call(s32[16]{0:T(128)} %ap_row.1, s32[16]{0:T(128)} %pr_row.1, s32[1]{0:T(128)S(6)} %copy.15.source, f32[1,12]{1,0:T(1,128)} %wavelet.1, s32[1,256]{1,0:T(1,128)} %receivers.1, f32[9,128,256]{2,1,0:T(8,128)} %bitcast.9, f32[128,256]{1,0:T(8,128)} %bitcast.10, ...), custom_call_target="tpu_custom_call" | custom-call | tf_op jit(solution)/shard_map/wave/pallas_call | solution.py:603
  106.2 2.9 %finish.1 = (f32[9,128,256]{2,1,0:T(8,128)}, f32[128,256]{1,0:T(8,128)}, f32[128,256]{1,0:T(8,128)}, f32[12,1,256]{2,1,0:T(1,128)}) custom-call(f32[10,256,128]{2,1,0:T(8,128)} %get-tuple-element.11.planes, f32[128,256]{1,0:T(8,128)} %get-tuple-element.12.owner, f32[12,256]{1,0:T(8,128)} %get-tuple-element.13.trace), custom_call_target="tpu_custom_call" | custom-call | tf_op jit(solution)/shard_map/finish/pallas_call | solution.py:664

commit v5 on v4

--- a/solution.py
+++ b/solution.py
@@ -60,22 +60,24 @@
     s_i = lax.axis_index("shot")
     t_i = lax.axis_index("tile")
 
-    def snake(i):
-        return jnp.where(i < 4, i, 11 - i)
-
-    d = snake(t_i)
     core = s_i % 2
     base = s_i - core
-    swapped = d % 2 == 1
-    role = base + (core + d) % 2
+    x_lo = t_i // 4
+    d = 2 * (t_i % 4) + core
+    role = base + x_lo
+    swapped = core != x_lo
+
+    def owner_of(shot, slab):
+        return (shot - shot % 2 + slab % 2, (shot % 2) * 4 + slab // 2)
+
     piece = (s_i + 2 * t_i) % 16
     piece_d = piece // 2
     half = piece % 2
     elsewhere = piece_d != d
     has_left = d > 0
     has_right = d < 7
-    left_id = (base + 1 - core, snake(jnp.maximum(d - 1, 0)))
-    right_id = (base + 1 - core, snake(jnp.minimum(d + 1, 7)))
+    left_id = owner_of(role, jnp.maximum(d - 1, 0))
+    right_id = owner_of(role, jnp.minimum(d + 1, 7))
 
     def remote(src, dst, send, recv, device):
         return pltpu.make_async_remote_copy(
@@ -162,29 +164,27 @@
     table.start()
 
     def move_wave(k):
-        to = 4 * ((t_i // 4 + k // 4) % 2) + (t_i + k) % 4
-        dd = snake(to)
+        dd = (d + k) % 8
         return remote(
             T.at[:, pl.ds(32 * dd, 32), :],
             RW.at[:, pl.ds(32 * t_i, 32), :],
             w_send.at[k],
             w_recv,
-            (base + (core + dd) % 2, to),
+            owner_of(s_i, dd),
         )
 
     waves = [move_wave(k) for k in WAVE_ORDER]
     wave_near = move_wave(0)
 
-    @pl.when(core == 0)
-    def _():
-        for i in (3, 0, 4, 1, 5, 2, 6):
+    @pl.when(jnp.logical_not(swapped))
+    def _():
+        for i in (0, 1, 2, 3, 4, 5, 6):
             waves[i].start()
 
-    @pl.when(core == 1)
+    @pl.when(swapped)
     def _():
         for i in (0, 1, 2):
             waves[i].start()
-
 
     pl.when(swapped)(wave_near.start)
 
@@ -233,7 +233,7 @@
             RM.at[:, pl.ds(32 * t_i + 16 * half, 16), :],
             n_send.at[k],
             n_recv,
-            (s - s % 2 + (s % 2 + piece_d) % 2, snake(piece_d)),
+            owner_of(s, piece_d),
         )
 
     deliver = [send_material(k) for k in range(16)]
@@ -249,7 +249,7 @@
         pltpu.make_async_copy(M.at[role], RM.at[:, pl.ds(32 * t_i + 16 * half, 16), :], n_recv).start()
 
 
-    @pl.when(core == 1)
+    @pl.when(swapped)
     def _():
         for i in (3, 4, 5, 6):
             waves[i].start()
@@ -482,7 +482,7 @@
             (role, t),
         )
 
-    homes = [[send_home(part, k) for k in (0,) + WAVE_ORDER] for part in range(2)]
+    homes = [[send_home(part, k) for k in (0, 4, 6, 5, 7, 1, 3, 2)] for part in range(2)]
 
     def start_home(part):
         for copy in homes[part][1:]:
@@ -533,6 +533,21 @@
 
     lax.fori_loop(0, STEPS, step, 0)
 
+    for n in range(STEPS):
+        TRS[n : n + 1, :] = TRB[n, 0:1, :]
+
+    def send_trace(k):
+        return remote(TRS, TRR.at[d], t_send.at[k], t_recv, (role, (t_i + k) % 8))
+
+    traces = [send_trace(k) for k in range(8)]
+    for copy in traces[1:]:
+        copy.start()
+    pl.when(swapped)(traces[0].start)
+
+    @pl.when(jnp.logical_not(swapped))
+    def _():
+        pltpu.make_async_copy(TRS, TRR.at[d], t_recv).start()
+
     for z in range(32):
         rows = pl.ds(z, 8, stride=32)
         for j, f in enumerate(WITH_Z):
@@ -541,21 +556,6 @@
             OB[f, rows, :] = SO[j, z]
         OB[9, rows, :] = IMG[z] * UNIT
     start_home(1)
-
-    for n in range(STEPS):
-        TRS[n : n + 1, :] = TRB[n, 0:1, :]
-
-    def send_trace(k):
-        return remote(TRS, TRR.at[d], t_send.at[k], t_recv, (role, (t_i + k) % 8))
-
-    traces = [send_trace(k) for k in range(8)]
-    for copy in traces[1:]:
-        copy.start()
-    pl.when(swapped)(traces[0].start)
-
-    @pl.when(jnp.logical_not(swapped))
-    def _():
-        pltpu.make_async_copy(TRS, TRR.at[d], t_recv).start()
 
     for copies in (spread, grads, owners, waves):
         for copy in copies:

time: 111 us -> 102 us (0.919)
  Pallas kernels: 108 us -> 99.8 us
    pallas_call x1, Pallas kernels: 105 us -> 96.9 us  [on_device(): pl.pallas_call(kernel, out_shape=(jax.ShapeDtypeStruct((10, 256, 128), F3...]
where the time goes in v5:
time: 102 us; the launch traced here: 101 us
  Pallas kernels  99.8 us (98%)
  between operations  1.29 us (1%)
    pallas_call x1, Pallas kernels, on_device(): pl.pallas_call(kernel, out_shape=(jax.ShapeDtypeStruct((10, 256, 128), F3...  96.9 us
    pallas_call x1, Pallas kernels, on_device(): pl.pallas_call(finish, out_shape=(jax.ShapeDtypeStruct((9, 128, 256), F32...  2.86 us

profile of v5, /device:TPU:2, one launch (start us, length us, event | category | flops | bytes accessed | tf_op | source)
XLA Modules:
  0.0 101.1 jit_solution(7232417448950468315)
XLA Ops:
  1.3 96.9 %wave.1 = (f32[10,256,128]{2,1,0:T(8,128)}, f32[128,256]{1,0:T(8,128)}, f32[12,256]{1,0:T(8,128)}) custom-call(s32[16]{0:T(128)} %ap_row.1, s32[16]{0:T(128)} %pr_row.1, s32[1]{0:T(128)S(6)} %copy.15.source, f32[1,12]{1,0:T(1,128)} %wavelet.1, s32[1,256]{1,0:T(1,128)} %receivers.1, f32[9,128,256]{2,1,0:T(8,128)} %bitcast.9, f32[128,256]{1,0:T(8,128)} %bitcast.10, ...), custom_call_target="tpu_custom_call" | custom-call | tf_op jit(solution)/shard_map/wave/pallas_call | solution.py:603
  98.2 2.9 %finish.1 = (f32[9,128,256]{2,1,0:T(8,128)}, f32[128,256]{1,0:T(8,128)}, f32[128,256]{1,0:T(8,128)}, f32[12,1,256]{2,1,0:T(1,128)}) custom-call(f32[10,256,128]{2,1,0:T(8,128)} %get-tuple-element.11.planes, f32[128,256]{1,0:T(8,128)} %get-tuple-element.12.owner, f32[12,256]{1,0:T(8,128)} %get-tuple-element.13.trace), custom_call_target="tpu_custom_call" | custom-call | tf_op jit(solution)/shard_map/finish/pallas_call | solution.py:664

commit v6 on v5

--- a/solution.py
+++ b/solution.py
@@ -261,8 +261,6 @@
             SZ[j, 4 + z] = RW[f, rows, :]
         for j, f in enumerate(IN_PLANE):
             SO[j, z] = RW[f, rows, :]
-        for j, f in enumerate(VELOCITY):
-            V[j, 4 + z] = RW[f, rows, :]
 
     def halo(par, part):
         def one(side, src, dst, device):
@@ -296,6 +294,9 @@
                 to_left.wait_recv()
 
     start_halo(0, 0)
+    for z in range(32):
+        for j, f in enumerate(VELOCITY):
+            V[j, 4 + z] = RW[f, pl.ds(z, 8, stride=32), :]
 
     pltpu.make_async_copy(RM, RM, n_recv).wait()
     for z in range(32):
@@ -311,10 +312,6 @@
     cell = (4 * sub + lane // 32) * 8192 + (lane % 32) * 256 + 32 * d
     where_source = PR[18:19, :].astype(jnp.int32)
     for z in range(32):
-        shear = RM[1, pl.ds(z, 8, stride=32), :] * (DT * UNIT)
-        L[z] = RM[0, pl.ds(z, 8, stride=32), :] * (DT * UNIT)
-        MU[z] = shear
-        MU2[z] = 2.0 * shear
         SRC[z] = jnp.where(cell + z == where_source, RM[2, pl.ds(z, 8, stride=32), :] * DT, 0.0)
 
     first = (sub == 0)[None]
@@ -460,6 +457,11 @@
 
     partial_velocity(0, PR[0:1, :])
     start_halo(0, 1)
+    for z in range(32):
+        shear = RM[1, pl.ds(z, 8, stride=32), :] * (DT * UNIT)
+        L[z] = RM[0, pl.ds(z, 8, stride=32), :] * (DT * UNIT)
+        MU[z] = shear
+        MU2[z] = 2.0 * shear
 
     @pl.when(has_left)
     def _():

time: 102 us -> 102 us (level)
  no operation moved by 1% of the time
where the time goes in v6:
time: 102 us; the launch traced here: 101 us
  Pallas kernels  99.5 us (98%)
  between operations  1.29 us (1%)
    pallas_call x1, Pallas kernels, on_device(): pl.pallas_call(kernel, out_shape=(jax.ShapeDtypeStruct((10, 256, 128), F3...  96.7 us
    pallas_call x1, Pallas kernels, on_device(): pl.pallas_call(finish, out_shape=(jax.ShapeDtypeStruct((9, 128, 256), F32...  2.86 us

profile of v6, /device:TPU:2, one launch (start us, length us, event | category | flops | bytes accessed | tf_op | source)
XLA Modules:
  0.0 100.8 jit_solution(17476617348837285164)
XLA Ops:
  1.3 96.7 %wave.1 = (f32[10,256,128]{2,1,0:T(8,128)}, f32[128,256]{1,0:T(8,128)}, f32[12,256]{1,0:T(8,128)}) custom-call(s32[16]{0:T(128)} %ap_row.1, s32[16]{0:T(128)} %pr_row.1, s32[1]{0:T(128)S(6)} %copy.15.source, f32[1,12]{1,0:T(1,128)} %wavelet.1, s32[1,256]{1,0:T(1,128)} %receivers.1, f32[9,128,256]{2,1,0:T(8,128)} %bitcast.9, f32[128,256]{1,0:T(8,128)} %bitcast.10, ...), custom_call_target="tpu_custom_call" | custom-call | tf_op jit(solution)/shard_map/wave/pallas_call | solution.py:605
  97.9 2.9 %finish.1 = (f32[9,128,256]{2,1,0:T(8,128)}, f32[128,256]{1,0:T(8,128)}, f32[128,256]{1,0:T(8,128)}, f32[12,1,256]{2,1,0:T(1,128)}) custom-call(f32[10,256,128]{2,1,0:T(8,128)} %get-tuple-element.11.planes, f32[128,256]{1,0:T(8,128)} %get-tuple-element.12.owner, f32[12,256]{1,0:T(8,128)} %get-tuple-element.13.trace), custom_call_target="tpu_custom_call" | custom-call | tf_op jit(solution)/shard_map/finish/pallas_call | solution.py:666

commit v7 on v6

--- a/solution.py
+++ b/solution.py
@@ -15,7 +15,7 @@
 DT = 0.2
 STEPS = 12
 
-WAVE_ORDER = (1, 3, 2, 4, 5, 7, 6)
+WAVE_ORDER = (4, 3, 5, 2, 6, 1, 7)
 
 VELOCITY = (0, 1, 2)
 WITH_Z = (7, 8, 5)
@@ -505,6 +505,16 @@
                 OB[f, rows, :] = V[j, 4 + z]
         start_home(0)
 
+    def rest_home():
+        for z in range(32):
+            rows = pl.ds(z, 8, stride=32)
+            for j, f in enumerate(WITH_Z):
+                OB[f, rows, :] = SZ[j, 4 + z]
+            for j, f in enumerate(IN_PLANE):
+                OB[f, rows, :] = SO[j, z]
+            OB[9, rows, :] = IMG[z] * UNIT
+        start_home(1)
+
     def step(n, carry):
         par = lax.rem(n, 2)
         amplitude = PR[pl.ds(n, 1), :]
@@ -524,6 +534,7 @@
 
         for z0 in (8, 16):
             stresses(z0)
+        pl.when(n == STEPS - 1)(rest_home)
         picked = jnp.dot(R1[...], split(V[2, 4:36].reshape(256, 128)), preferred_element_type=F32)
         picked = (picked * L2[...]).astype(BF16)
         TRB[n] = lax.dot_general(
@@ -550,14 +561,6 @@
     def _():
         pltpu.make_async_copy(TRS, TRR.at[d], t_recv).start()
 
-    for z in range(32):
-        rows = pl.ds(z, 8, stride=32)
-        for j, f in enumerate(WITH_Z):
-            OB[f, rows, :] = SZ[j, 4 + z]
-        for j, f in enumerate(IN_PLANE):
-            OB[f, rows, :] = SO[j, z]
-        OB[9, rows, :] = IMG[z] * UNIT
-    start_home(1)
 
     for copies in (spread, grads, owners, waves):
         for copy in copies:

time: 102 us -> 103 us (level)
  Pallas kernels: 99.5 us -> 101 us
    pallas_call x1, Pallas kernels: 96.7 us -> 97.7 us  [on_device(): pl.pallas_call(kernel, out_shape=(jax.ShapeDtypeStruct((10, 256, 128), F3...]
where the time goes in v7:
time: 103 us; the launch traced here: 102 us
  Pallas kernels  101 us (98%)
  between operations  1.29 us (1%)
    pallas_call x1, Pallas kernels, on_device(): pl.pallas_call(kernel, out_shape=(jax.ShapeDtypeStruct((10, 256, 128), F3...  97.7 us
    pallas_call x1, Pallas kernels, on_device(): pl.pallas_call(finish, out_shape=(jax.ShapeDtypeStruct((9, 128, 256), F32...  2.86 us

profile of v7, /device:TPU:2, one launch (start us, length us, event | category | flops | bytes accessed | tf_op | source)
XLA Modules:
  0.0 101.9 jit_solution(14219699755901893265)
XLA Ops:
  1.3 97.7 %wave.1 = (f32[10,256,128]{2,1,0:T(8,128)}, f32[128,256]{1,0:T(8,128)}, f32[12,256]{1,0:T(8,128)}) custom-call(s32[16]{0:T(128)} %ap_row.1, s32[16]{0:T(128)} %pr_row.1, s32[1]{0:T(128)S(6)} %copy.15.source, f32[1,12]{1,0:T(1,128)} %wavelet.1, s32[1,256]{1,0:T(1,128)} %receivers.1, f32[9,128,256]{2,1,0:T(8,128)} %bitcast.9, f32[128,256]{1,0:T(8,128)} %bitcast.10, ...), custom_call_target="tpu_custom_call" | custom-call | tf_op jit(solution)/shard_map/wave/pallas_call | solution.py:608
  99.0 2.9 %finish.1 = (f32[9,128,256]{2,1,0:T(8,128)}, f32[128,256]{1,0:T(8,128)}, f32[128,256]{1,0:T(8,128)}, f32[12,1,256]{2,1,0:T(1,128)}) custom-call(f32[10,256,128]{2,1,0:T(8,128)} %get-tuple-element.11.planes, f32[128,256]{1,0:T(8,128)} %get-tuple-element.12.owner, f32[12,256]{1,0:T(8,128)} %get-tuple-element.13.trace), custom_call_target="tpu_custom_call" | custom-call | tf_op jit(solution)/shard_map/finish/pallas_call | solution.py:669
